TPU v7x, 128 devices: a whole 4x4x4 slice. The times are simulated.
128 devices in a mesh: gx: 8 (over z, core), gy: 4 (over x), gz: 4 (over y).
Axes of the slice: x: 4, y: 4, z: 4, core: 2. Of those that a mesh axis runs over, the one named last changes fastest.
Arguments:
- snapshots: float32 [16, 128, 128, 1024], P(None, 'gx', 'gy', 'gz'), as said below
- diffusivity: float32 [128, 128, 1024], P('gx', 'gy', 'gz'), may hold values from 0.02 to 0.16
Outputs:
- shifted: float32 [16, 128, 128, 1024], P(None, 'gx', 'gy', 'gz')
- reduced: float32 [16, 16], replicated
- sigmas: float32 [16], replicated
Inputs may be any that keep to these rules, and one draw needn't show every extreme that they name: `snapshots`: real values.
All inputs are finite; a program needn't handle non-finite values.
Results may differ from a plain program's by a relative error of at most 0.0003.
Values sent between devices are 32-bit elements; how exact they have to be, the bound alone decides.
A program may use at most 128 MiB of HBM per device.

v0:
```python
import jax
import jax.numpy as jnp
import numpy as np
from jax import lax
from jax.sharding import PartitionSpec as P

SNAPS = 16
RANK = 12
SWEEPS = 6


def extended(block, sides, width):
    for axis, dim in sides:
        count = lax.axis_size(axis)
        forward = [(i, i + 1) for i in range(count - 1)]
        forward.append((count - 1, 0))
        backward = [(target, source) for source, target in forward]
        low = lax.ppermute(
            lax.slice_in_dim(block, block.shape[dim] - width, None, axis=dim), axis, forward
        )
        high = lax.ppermute(lax.slice_in_dim(block, 0, width, axis=dim), axis, backward)
        block = jnp.concatenate([low, block, high], axis=dim)
    return block


def round_pairs(count):
    players = list(range(count))
    firsts = []
    seconds = []
    for turn in range(count - 1):
        firsts.append([players[i] for i in range(count // 2)])
        seconds.append([players[count - 1 - i] for i in range(count // 2)])
        players = [players[0]] + [players[-1]] + players[1:-1]
    return (np.array(firsts, dtype=np.int32), np.array(seconds, dtype=np.int32))


def jacobi_eigen(small):
    count = small.shape[0]
    first_np, second_np = round_pairs(count)
    firsts = jnp.asarray(first_np)
    seconds = jnp.asarray(second_np)
    eye = jnp.eye(count, dtype=jnp.float32)
    high = lax.Precision.HIGHEST

    def turn(step, carry):
        mat, vecs = carry
        row = step % (count - 1)
        pidx = firsts[row]
        qidx = seconds[row]
        app = mat[pidx, pidx]
        aqq = mat[qidx, qidx]
        apq = mat[pidx, qidx]
        tau = aqq - app
        sgn = jnp.where(tau >= 0, 1.0, -1.0).astype(jnp.float32)
        denom = jnp.abs(tau) + jnp.sqrt(tau * tau + 4.0 * apq * apq)
        tangent = jnp.where(denom > 0, 2.0 * apq * sgn / jnp.where(denom > 0, denom, 1.0), 0.0)
        cosine = 1.0 / jnp.sqrt(1.0 + tangent * tangent)
        sine = tangent * cosine
        onep = jax.nn.one_hot(pidx, count, dtype=jnp.float32)
        oneq = jax.nn.one_hot(qidx, count, dtype=jnp.float32)
        rot = eye + jnp.dot(onep.T, (cosine - 1.0)[:, None] * onep, precision=high)
        rot = rot + jnp.dot(oneq.T, (cosine - 1.0)[:, None] * oneq, precision=high)
        rot = rot + jnp.dot(onep.T, sine[:, None] * oneq, precision=high)
        rot = rot - jnp.dot(oneq.T, sine[:, None] * onep, precision=high)
        mat = jnp.dot(jnp.dot(rot.T, mat, precision=high), rot, precision=high)
        vecs = jnp.dot(vecs, rot, precision=high)
        return (mat, vecs)

    mat, vecs = lax.fori_loop(0, SWEEPS * (count - 1), turn, (small, eye))
    return (jnp.diagonal(mat), vecs)


def factor_pair(gram, cross):
    lower = jnp.linalg.cholesky(gram)
    proj = lax.linalg.triangular_solve(lower, cross, left_side=True, lower=True)
    return (lower.T, proj)


def finish(upper, proj, ncell):
    high = lax.Precision.HIGHEST
    small = jnp.dot(upper, upper.T, precision=high) / ncell
    lam, vecs = jacobi_eigen(small)
    ordered = jnp.sort(lam)[::-1]
    sigmas = jnp.sqrt(ordered)
    keep = (lam >= ordered[RANK - 1]).astype(jnp.float32)
    projector = jnp.dot(vecs * keep[None, :], vecs.T, precision=high)
    inverse = jnp.dot(vecs * (keep / lam)[None, :], vecs.T, precision=high) / ncell
    reduced = jnp.dot(jnp.dot(projector, proj, precision=high), upper.T, precision=high)
    reduced = jnp.dot(reduced, inverse, precision=high)
    return (reduced, sigmas)


def view(padded, dim, offset):
    leading = tuple((slice(None) for lead_pos in range(padded.ndim - 3)))
    parts = [slice(2, padded.shape[padded.ndim - 3 + axis_pos] - 2) for axis_pos in range(3)]
    length = padded.shape[padded.ndim - 3 + dim] - 4
    parts[dim] = slice(2 + offset, 2 + offset + length)
    return padded[leading + tuple(parts)]


def advance(padded, diffusivity):
    field = view(padded, 0, 0)
    lap = -6.0 * field
    for dim in range(3):
        lap = lap + view(padded, dim, 1) + view(padded, dim, -1)

    def slope(dim):
        return (
            8.0 * (view(padded, dim, 1) - view(padded, dim, -1))
            - (view(padded, dim, 2) - view(padded, dim, -2))
        ) / 12.0

    return (
        field
        + diffusivity * lap
        - (0.3 + 0.02 * field) * slope(2)
        - 0.2 * slope(0)
        - 0.15 * slope(1)
    )


def shards(snapshots, diffusivity):
    high = lax.Precision.HIGHEST

    def one_field(index, collected):
        field = lax.dynamic_index_in_dim(snapshots, index, 0, keepdims=False)
        padded = extended(field, (("gx", 0), ("gy", 1), ("gz", 2)), 2)
        return lax.dynamic_update_index_in_dim(collected, advance(padded, diffusivity), index, 0)

    shifted = lax.fori_loop(0, snapshots.shape[0], one_field, jnp.zeros_like(snapshots))
    flat_x = snapshots.reshape(SNAPS, -1)
    flat_y = shifted.reshape(SNAPS, -1)
    gram = jnp.dot(flat_x, flat_x.T, precision=high)
    cross = jnp.dot(flat_x, flat_y.T, precision=high)
    ncell = float(flat_x.shape[1] * lax.axis_size("gx") * lax.axis_size("gy") * lax.axis_size("gz"))
    gram, cross = lax.psum((gram, cross), ("gx", "gy", "gz"))
    upper, proj = factor_pair(gram, cross)
    reduced, sigmas = finish(upper, proj, ncell)
    return (shifted, reduced, sigmas)


def solution(mesh):
    placed = (P(None, "gx", "gy", "gz"), P("gx", "gy", "gz"))
    return jax.shard_map(
        shards,
        mesh=mesh,
        in_specs=placed,
        out_specs=(P(None, "gx", "gy", "gz"), P(), P()),
        check_vma=False,
    )
```

profile of v0, /device:TPU:0, one launch (start us, length us, event | category | flops | bytes accessed | tf_op | source)
XLA Modules:
  0.0 980.5 jit_solution(14451856743499966787)
XLA Ops:
  0.6 411.3 %while.34 = (s32[]{:T(128)}, f32[16,16,32,256]{3,2,1,0:T(8,128)}, f32[16,16,32,256]{3,2,1,0:T(8,128)}, f32[16,32,256]{2,1,0:T(8,128)}, s32[]{:T(128)}, /*index=5*/s32[]{:T(128)}, s32[]{}) while((s32[]{:T(128)}, f32[16,16,32,256]{3,2,1,0:T(8,128)}, f32[16,16,32,256]{3,2,1,0:T(8,128)}, f32[16,32,256]{2,1,0:T(8,128)}, s32[]{:T(128)}, ...), condition=%wide.region_1.2_spmd, body=%wide.region_0.1_spmd.sunk | while | flops 8900611 | bytes 10468449 | solution.py:130
  21.8 5.8 collective-permute-done.4
  48.5 5.8 collective-permute-done.4
  73.7 5.8 collective-permute-done.4
  98.2 6.3 collective-permute-done.4
  104.5 3.8 fusion.118
  123.4 6.9 collective-permute-done.4
  130.3 3.8 fusion.118
  149.1 6.6 collective-permute-done.4
  155.7 3.8 fusion.118
  174.6 6.4 collective-permute-done.4
  200.0 5.8 collective-permute-done.4
  224.6 6.5 collective-permute-done.4
  250.0 6.9 collective-permute-done.4
  275.7 6.5 collective-permute-done.4
  301.1 5.8 collective-permute-done.4
  325.9 6.4 collective-permute-done.4
  351.1 6.9 collective-permute-done.4
  376.9 6.5 collective-permute-done.4
  402.3 5.8 collective-permute-done.4
  411.9 25.4 %fusion.56 = f32[16,16]{0,1:T(8,128)S(1)} fusion(f32[16,16,32,256]{3,2,1,0:T(8,128)} %get-tuple-element.458, f32[16,16,32,256]{3,2,1,0:T(8,128)} %get-tuple-element.270), kind=kOutput, calls=%fused_computation.108 | convolution fusion | flops 402653184 | bytes 16778240 | tf_op jit(solution)/shard_map/dot_general | solution.py:134
  437.4 14.0 %fusion.53 = f32[16,16]{0,1:T(8,128)S(1)} fusion(f32[16,16,32,256]{3,2,1,0:T(8,128)S(1)} %copy-done), kind=kOutput, calls=%fused_computation.105 | convolution fusion | flops 402653184 | bytes 8389632 | tf_op jit(solution)/shard_map/dot_general | solution.py:133
  451.4 65.1 %all-reduce = (f32[16,16]{0,1:T(8,128)S(1)}, f32[16,16]{0,1:T(8,128)S(1)}) all-reduce(f32[16,16]{0,1:T(8,128)S(1)} %fusion.53, f32[16,16]{0,1:T(8,128)S(1)} %fusion.56), channel_id=1, replica_groups=mesh['gx'=8,'gy'=4,'gz'=4] {'gx','gy','gz'}, use_global_device_ids=true, to_apply=%region_2.3 | all-reduce | flops 512 | bytes 4096 | tf_op jit(solution)/shard_map/psum | solution.py:136
  519.6 452.1 %while.35 = (s32[]{:T(128)}, f32[16,16]{1,0:T(8,128)S(1)}, f32[16,16]{0,1:T(8,128)S(1)}, s32[]{:T(128)}, s32[15,8]{1,0:T(8,128)}, /*index=5*/s32[]{:T(128)}, s32[]{:T(128)}, s32[15,8]{1,0:T(8,128)}) while((s32[]{:T(128)}, f32[16,16]{1,0:T(8,128)S(1)}, f32[16,16]{0,1:T(8,128)S(1)}, s32[]{:T(128)}, ...), condition=%wide.region_6.7_spmd.clone.clone, body=%wide.region_5.6_spmd.sunk.clone.clone.sunk | while | flops 249131 | bytes 19833 | solution.py:69
  (1663 shorter events, 760.9 us)
Async XLA Ops:
  18.4 9.2 collective-permute-start.4
  45.1 9.2 collective-permute-start.4
  70.2 9.2 collective-permute-start.4
  94.7 9.8 %collective-permute-start.4 = (f32[20,36,2]{2,1,0:T(8,128)S(1)}, f32[20,36,2]{2,1,0:T(8,128)S(1)}, u32[]{:S(2)}, u32[]{:S(2)}) collective-permute-start(f32[20,36,2]{2,1,0:T(8,128)S(1)} %get-tuple-element.401), channel_id=1, source_target_pairs={{0,1},{1,2},{2,3},{3,0},{4,5},{5,6},{6,7},{7,4},{8,9},{9,10},{10,1... | collective-permute-start | bytes 17288 | tf_op jit(solution)/shard_map/while/body/eval_jaxpr/ppermute | solution.py:18
  96.0 8.6 collective-permute-start.5
  119.9 10.4 %collective-permute-start.4 = (f32[20,36,2]{2,1,0:T(8,128)S(1)}, f32[20,36,2]{2,1,0:T(8,128)S(1)}, u32[]{:S(2)}, u32[]{:S(2)}) collective-permute-start(f32[20,36,2]{2,1,0:T(8,128)S(1)} %get-tuple-element.401), channel_id=1, source_target_pairs={{0,1},{1,2},{2,3},{3,0},{4,5},{5,6},{6,7},{7,4},{8,9},{9,10},{10,1... | collective-permute-start | bytes 17288 | tf_op jit(solution)/shard_map/while/body/eval_jaxpr/ppermute | solution.py:18
  121.3 9.0 collective-permute-start.5
  145.7 10.1 %collective-permute-start.4 = (f32[20,36,2]{2,1,0:T(8,128)S(1)}, f32[20,36,2]{2,1,0:T(8,128)S(1)}, u32[]{:S(2)}, u32[]{:S(2)}) collective-permute-start(f32[20,36,2]{2,1,0:T(8,128)S(1)} %get-tuple-element.401), channel_id=1, source_target_pairs={{0,1},{1,2},{2,3},{3,0},{4,5},{5,6},{6,7},{7,4},{8,9},{9,10},{10,1... | collective-permute-start | bytes 17288 | tf_op jit(solution)/shard_map/while/body/eval_jaxpr/ppermute | solution.py:18
  147.0 8.7 collective-permute-start.5
  171.1 9.9 %collective-permute-start.4 = (f32[20,36,2]{2,1,0:T(8,128)S(1)}, f32[20,36,2]{2,1,0:T(8,128)S(1)}, u32[]{:S(2)}, u32[]{:S(2)}) collective-permute-start(f32[20,36,2]{2,1,0:T(8,128)S(1)} %get-tuple-element.401), channel_id=1, source_target_pairs={{0,1},{1,2},{2,3},{3,0},{4,5},{5,6},{6,7},{7,4},{8,9},{9,10},{10,1... | collective-permute-start | bytes 17288 | tf_op jit(solution)/shard_map/while/body/eval_jaxpr/ppermute | solution.py:18
  172.5 8.5 collective-permute-start.5
  196.6 9.2 collective-permute-start.4
  221.1 10.0 %collective-permute-start.4 = (f32[20,36,2]{2,1,0:T(8,128)S(1)}, f32[20,36,2]{2,1,0:T(8,128)S(1)}, u32[]{:S(2)}, u32[]{:S(2)}) collective-permute-start(f32[20,36,2]{2,1,0:T(8,128)S(1)} %get-tuple-element.401), channel_id=1, source_target_pairs={{0,1},{1,2},{2,3},{3,0},{4,5},{5,6},{6,7},{7,4},{8,9},{9,10},{10,1... | collective-permute-start | bytes 17288 | tf_op jit(solution)/shard_map/while/body/eval_jaxpr/ppermute | solution.py:18
  246.5 10.4 %collective-permute-start.4 = (f32[20,36,2]{2,1,0:T(8,128)S(1)}, f32[20,36,2]{2,1,0:T(8,128)S(1)}, u32[]{:S(2)}, u32[]{:S(2)}) collective-permute-start(f32[20,36,2]{2,1,0:T(8,128)S(1)} %get-tuple-element.401), channel_id=1, source_target_pairs={{0,1},{1,2},{2,3},{3,0},{4,5},{5,6},{6,7},{7,4},{8,9},{9,10},{10,1... | collective-permute-start | bytes 17288 | tf_op jit(solution)/shard_map/while/body/eval_jaxpr/ppermute | solution.py:18
  247.9 9.0 collective-permute-start.5
  272.3 9.9 %collective-permute-start.4 = (f32[20,36,2]{2,1,0:T(8,128)S(1)}, f32[20,36,2]{2,1,0:T(8,128)S(1)}, u32[]{:S(2)}, u32[]{:S(2)}) collective-permute-start(f32[20,36,2]{2,1,0:T(8,128)S(1)} %get-tuple-element.401), channel_id=1, source_target_pairs={{0,1},{1,2},{2,3},{3,0},{4,5},{5,6},{6,7},{7,4},{8,9},{9,10},{10,1... | collective-permute-start | bytes 17288 | tf_op jit(solution)/shard_map/while/body/eval_jaxpr/ppermute | solution.py:18
  273.6 8.6 collective-permute-start.5
  297.7 9.2 collective-permute-start.4
  322.5 9.8 %collective-permute-start.4 = (f32[20,36,2]{2,1,0:T(8,128)S(1)}, f32[20,36,2]{2,1,0:T(8,128)S(1)}, u32[]{:S(2)}, u32[]{:S(2)}) collective-permute-start(f32[20,36,2]{2,1,0:T(8,128)S(1)} %get-tuple-element.401), channel_id=1, source_target_pairs={{0,1},{1,2},{2,3},{3,0},{4,5},{5,6},{6,7},{7,4},{8,9},{9,10},{10,1... | collective-permute-start | bytes 17288 | tf_op jit(solution)/shard_map/while/body/eval_jaxpr/ppermute | solution.py:18
  347.7 10.4 %collective-permute-start.4 = (f32[20,36,2]{2,1,0:T(8,128)S(1)}, f32[20,36,2]{2,1,0:T(8,128)S(1)}, u32[]{:S(2)}, u32[]{:S(2)}) collective-permute-start(f32[20,36,2]{2,1,0:T(8,128)S(1)} %get-tuple-element.401), channel_id=1, source_target_pairs={{0,1},{1,2},{2,3},{3,0},{4,5},{5,6},{6,7},{7,4},{8,9},{9,10},{10,1... | collective-permute-start | bytes 17288 | tf_op jit(solution)/shard_map/while/body/eval_jaxpr/ppermute | solution.py:18
  349.1 9.0 collective-permute-start.5
  373.5 9.9 %collective-permute-start.4 = (f32[20,36,2]{2,1,0:T(8,128)S(1)}, f32[20,36,2]{2,1,0:T(8,128)S(1)}, u32[]{:S(2)}, u32[]{:S(2)}) collective-permute-start(f32[20,36,2]{2,1,0:T(8,128)S(1)} %get-tuple-element.401), channel_id=1, source_target_pairs={{0,1},{1,2},{2,3},{3,0},{4,5},{5,6},{6,7},{7,4},{8,9},{9,10},{10,1... | collective-permute-start | bytes 17288 | tf_op jit(solution)/shard_map/while/body/eval_jaxpr/ppermute | solution.py:18
  374.8 8.6 collective-permute-start.5
  398.9 9.2 collective-permute-start.4
  (73 other events, 353.7 us)
where the time goes:
time: 993 us; the launch traced here: 981 us
  local copies, waits for them, and re-layouts  275 us (28%)
  waiting for transfers between devices  213 us (21%)
  matrix products  186 us (19%)
  other arithmetic  139 us (14%)
  starting transfers between devices  99.3 us (10%)
  blocking collectives  65.1 us (7%)
    ppermute x48, waiting for transfers between devices, extended(): lax.ppermute(lax.slice_in_dim(block, block.shape[dim] - width, None, axis...  175 us
    concatenate x90, other arithmetic, turn(): app = mat[pidx, pidx]  65.6 us
    psum x1, blocking collectives, shards(): gram, cross = lax.psum((gram, cross), ('gx', 'gy', 'gz'))  65.1 us
    eq x90, local copies, waits for them, and re-layouts, turn(): onep = jax.nn.one_hot(pidx, count, dtype=jnp.float32)  64.9 us
    dynamic_update_slice x16, other arithmetic, one_field(): lax.dynamic_update_index_in_dim(collected, advance(padded, diffusivity),...  60 us
    gather x90, local copies, waits for them, and re-layouts, turn(): aqq = mat[qidx, qidx]  58.1 us
    gather x90, local copies, waits for them, and re-layouts, turn(): app = mat[pidx, pidx]  58.1 us
    gather x90, local copies, waits for them, and re-layouts, turn(): apq = mat[pidx, qidx]  57.4 us
  transfers between devices with their start and end apart: 96, of which 84 were waited for; matrix products, arithmetic and copies ran while one was open for 2% of the time, Pallas kernels for 0%

commit v1 on v0

v1 whole, which is shorter than its diff:
```python
import functools

import jax
import jax.numpy as jnp
from jax import lax
from jax.experimental import pallas as pl
from jax.experimental.pallas import tpu as pltpu
from jax.sharding import PartitionSpec as P

SNAPS = 16
RANK = 12
SWEEPS = 6
HIGH = lax.Precision.HIGHEST
F32 = jnp.float32
BF16 = jnp.bfloat16
MESH = pl.DeviceIdType.MESH
AXES = ("gx", "gy", "gz")


def peers(sizes):
    found = []
    for axis, count in zip(AXES, sizes):
        for step in range(1, count):
            found.append((axis, step, lax.rem(lax.axis_index(axis) + step, count)))
    return found


def enter(sizes):
    barrier = pltpu.get_barrier_semaphore()
    known = peers(sizes)
    for axis, _, target in known:
        pl.semaphore_signal(barrier, inc=1, device_id={axis: target}, device_id_type=MESH)
    pl.semaphore_wait(barrier, len(known))


def pack_square(square):
    return jnp.concatenate([square[0:8], square[8:16]], axis=1)


def unpack_square(packed):
    return jnp.concatenate([packed[:, 0:16], packed[:, 16:32]], axis=0)


def sum_over_mesh(sizes, value, slots, send_sems, recv_sems):
    at = 0
    for place, (axis, count) in enumerate(zip(AXES, sizes)):
        me = lax.axis_index(axis)
        base = 8 * place
        slots[base + me, :, 0:32] = value
        copies = []
        for step in range(1, count):
            target = lax.rem(me + step, count)
            copy = pltpu.make_async_remote_copy(
                src_ref=slots.at[base + me],
                dst_ref=slots.at[base + me],
                send_sem=send_sems.at[at],
                recv_sem=recv_sems.at[at],
                device_id={axis: target},
                device_id_type=MESH,
            )
            copy.start()
            copies.append(copy)
            at += 1
        for copy in copies:
            copy.wait()
        value = slots[base, :, 0:32]
        for slot in range(1, count):
            value = value + slots[base + slot, :, 0:32]
    return value


def halves(block):
    high = block.astype(BF16)
    return high, (block - high.astype(F32)).astype(BF16)


def fold(total, groups):
    sub = lax.broadcasted_iota(jnp.int32, (8, 256), 0)
    lane = lax.broadcasted_iota(jnp.int32, (8, 256), 1)
    same = (sub == lane % 8).astype(F32)
    rows = jnp.sum(total.reshape(groups * 16, 8, 256) * same[None], axis=1)
    pick = (
        lax.broadcasted_iota(jnp.int32, (256, 32), 0) // 8
        == lax.broadcasted_iota(jnp.int32, (256, 32), 1)
    ).astype(F32)
    return jnp.dot(rows, pick, precision=HIGH, preferred_element_type=F32)


NT = (((1,), (1,)), ((), ()))
TN = (((0,), (0,)), ((), ()))


def exchange_kernel(
    sizes, snap, xlo, xhi, ylo, yhi, zlo, zhi, gram,
    field, yplo, yphi, zplo, zphi, total, slots,
    load_sem, xs, xr, ys, yr, zs, zr, gs, gr,
):
    planes = field.shape[0]
    parts = 4
    each = planes // parts
    for x in range(planes):
        pltpu.make_async_copy(snap.at[:, x], field.at[x], load_sem.at[x]).start()
    enter(sizes)
    near = {}
    for axis, count in zip(AXES, sizes):
        me = lax.axis_index(axis)
        near[axis] = (lax.rem(me + count - 1, count), lax.rem(me + 1, count))

    def remote(src, dst, send, recv, axis, side):
        copy = pltpu.make_async_remote_copy(
            src_ref=src, dst_ref=dst, send_sem=send, recv_sem=recv,
            device_id={axis: near[axis][side]}, device_id_type=MESH,
        )
        copy.start()
        return copy

    copies = [
        remote(snap.at[:, 0:2], xhi, xs.at[0], xr.at[0], "gx", 0),
        remote(snap.at[:, planes - 2:planes], xlo, xs.at[1], xr.at[1], "gx", 1),
    ]
    lane = lax.broadcasted_iota(jnp.int32, (32, 128), 1)

    def plane(x, carry):
        pltpu.make_async_copy(snap.at[:, x], field.at[x], load_sem.at[x]).wait()
        left = jnp.zeros((32, 128), F32)
        right = jnp.zeros((32, 128), F32)
        for k in range(SNAPS):
            yplo[x, 2 * k:2 * k + 2, :] = field[x, k, 0:2, :]
            yphi[x, 2 * k:2 * k + 2, :] = field[x, k, 30:32, :]
            head = field[x, k, :, 0:128]
            tail = field[x, k, :, 128:256]
            if k:
                head = pltpu.roll(head, 8 * k, 1)
                tail = pltpu.roll(tail, 8 * k, 1)
            left = jnp.where((lane >= 8 * k) & (lane < 8 * k + 2), head, left)
            low = (8 * k - 2) % 128
            right = jnp.where((lane >= low) & (lane < low + 2), tail, right)
        zplo[x] = left
        zphi[x] = right
        return carry

    def inner(x, carry):
        highs, lows = [], []
        for a in range(4):
            high, low = halves(field[x, :, 8 * a:8 * a + 8, :].reshape(128, 256))
            highs.append(high)
            lows.append(low)
        high = jnp.concatenate(highs, axis=1)
        both = jnp.concatenate([high, jnp.concatenate(lows, axis=1)], axis=0)
        total[...] += lax.dot_general(both, both, NT, preferred_element_type=F32)
        return carry

    total[...] = jnp.zeros_like(total)
    for part in range(parts):
        span = pl.ds(part * each, each)
        lax.fori_loop(part * each, (part + 1) * each, plane, 0)
        copies += [
            remote(yplo.at[span], yhi.at[span], ys.at[2 * part], yr.at[2 * part], "gy", 0),
            remote(yphi.at[span], ylo.at[span], ys.at[2 * part + 1], yr.at[2 * part + 1], "gy", 1),
            remote(zplo.at[span], zhi.at[span], zs.at[2 * part], zr.at[2 * part], "gz", 0),
            remote(zphi.at[span], zlo.at[span], zs.at[2 * part + 1], zr.at[2 * part + 1], "gz", 1),
        ]
    lax.fori_loop(0, planes, inner, 0)
    small = fold(total[...], 2)
    mine = (small[0:16, 0:16] + small[16:32, 16:32]) + (small[0:16, 16:32] + small[16:32, 0:16])
    gram[...] = unpack_square(sum_over_mesh(sizes, pack_square(mine), slots, gs, gr))
    for copy in copies:
        copy.wait()


def factor(gram):
    row = lax.broadcasted_iota(jnp.int32, (16, 32), 0)
    col = lax.broadcasted_iota(jnp.int32, (16, 32), 1)
    mat = jnp.concatenate([gram, (row == col).astype(F32)[:, 0:16]], axis=1)
    for j in range(16):
        scale = lax.rsqrt(mat[j:j + 1, j:j + 1])
        top = mat[j:j + 1, :] * scale
        side = jnp.where(row[:, 0:1] > j, mat[:, j:j + 1] * scale, 0.0)
        mat = jnp.where(row == j, top, mat - side * top)
    upper = jnp.where(col[:, 0:16] >= row[:, 0:16], mat[:, 0:16], 0.0)
    return upper, mat[:, 16:32]


def jacobi_round(first, second):
    lane = lax.broadcasted_iota(jnp.int32, (8, 32), 1)
    sub = lax.broadcasted_iota(jnp.int32, (8, 32), 0)
    inside = lane < 16
    masked_first = jnp.where(inside, first, 0.0)
    masked_second = jnp.where(inside, second, 0.0)
    app = jnp.sum(masked_first * first, axis=1, keepdims=True)
    aqq = jnp.sum(masked_second * second, axis=1, keepdims=True)
    apq = jnp.sum(masked_first * second, axis=1, keepdims=True)
    tau = aqq - app
    square = tau * tau + 4.0 * apq * apq
    live = square > 0
    inverse = lax.rsqrt(jnp.where(live, square, 1.0))
    cos2 = 0.5 + 0.5 * jnp.abs(tau) * inverse
    root = lax.rsqrt(cos2)
    cosine = jnp.where(live, cos2 * root, 1.0)
    signed = jnp.where(tau >= 0, apq, -apq)
    sine = jnp.where(live, signed * inverse * root, 0.0)
    new_first = cosine * first - sine * second
    new_second = sine * first + cosine * second
    down = pltpu.roll(new_first, 1, 0)
    up = pltpu.roll(new_second, 7, 0)
    entering = pltpu.roll(new_second, 1, 0)
    top = jnp.where(sub == 0, new_first, jnp.where(sub == 1, entering, down))
    bottom = jnp.where(sub == 7, new_first, up)
    return top, bottom


def jacobi_start(upper):
    eye = (
        lax.broadcasted_iota(jnp.int32, (16, 16), 0) == lax.broadcasted_iota(jnp.int32, (16, 16), 1)
    ).astype(F32)
    both = jnp.concatenate([upper, eye], axis=1)
    return both[0:8], jnp.concatenate([both[i:i + 1] for i in range(15, 7, -1)], axis=0)


def spectrum(first, second, norm, ncell, upper, lower_inverse):
    both = jnp.concatenate([first, second], axis=0)
    scaled = both[:, 0:16]
    vecs = both[:, 16:32]
    lam = jnp.sum(scaled * scaled, axis=1, keepdims=True)
    row = lax.broadcasted_iota(jnp.int32, (16, 16), 0)
    col = lax.broadcasted_iota(jnp.int32, (16, 16), 1)
    along = jnp.sum(jnp.where(row == col, lam, 0.0), axis=0, keepdims=True)
    above = (along > lam).astype(F32)
    ties = ((along == lam) & (col < row)).astype(F32)
    greater = jnp.sum(above, axis=1, keepdims=True)
    keep = (greater < RANK - 0.5).astype(F32)
    place = greater + jnp.sum(ties, axis=1, keepdims=True)
    sigma = jnp.sqrt(lam * (norm / ncell))
    sigmas = jnp.sum(jnp.where(place == col.astype(F32), sigma, 0.0), axis=0, keepdims=True)
    proj = lax.dot_general(vecs * keep, vecs, TN, precision=HIGH, preferred_element_type=F32)
    weights = keep / (lam * norm)
    inverse = lax.dot_general(vecs * weights, vecs, TN, precision=HIGH, preferred_element_type=F32)
    before = jnp.dot(proj, lower_inverse, precision=HIGH, preferred_element_type=F32)
    after = lax.dot_general(upper, inverse, TN, precision=HIGH, preferred_element_type=F32)
    return before, after, sigmas


def shift_kernel(
    ncell, snap, diff, xlo, xhi, ylo, yhi, zlo, zhi, gram,
    out, crossing, before, after, sigmas,
    field, total, sems,
):
    x = pl.program_id(0)
    planes = pl.num_programs(0)
    static_planes = field.shape[0] - 4

    def load(p, half):
        lanes = pl.ds(half * 128, 128)
        return pltpu.make_async_copy(
            snap.at[:, p, :, lanes], field.at[p + 2, :, half, pl.ds(8, 32)], sems.at[p + 2, half]
        )

    def edge(side, p, half):
        lanes = pl.ds(half * 128, 128)
        source = (xlo, xhi)[side]
        slot = p if side == 0 else static_planes + 2 + p
        return pltpu.make_async_copy(
            source.at[:, p, :, lanes], field.at[slot, :, half, pl.ds(8, 32)], sems.at[slot, half]
        )

    @pl.when(x == 0)
    def _():
        total[...] = jnp.zeros_like(total)
        for half in range(2):
            for p in range(2):
                edge(0, p, half).start()
        for p in range(static_planes):
            for half in range(2):
                load(p, half).start()
        for half in range(2):
            for p in range(2):
                edge(1, p, half).start()
        for half in range(2):
            for p in range(2):
                edge(0, p, half).wait()
                load(p, half).wait()

    @pl.when(x < planes - 2)
    def _():
        for half in range(2):
            load(x + 2, half).wait()

    @pl.when(x >= planes - 2)
    def _():
        for half in range(2):
            edge(1, x - (planes - 2), half).wait()

    lane = lax.broadcasted_iota(jnp.int32, (32, 128), 1)
    group = lane % 8
    side = jnp.where(group < 4, zhi[0], zlo[0])
    for k in range(SNAPS):
        for half in range(2):
            lanes = pl.ds(half * 128, 128)
            field[x + 2, k, half, 6:8, :] = ylo[0, 2 * k:2 * k + 2, lanes]
            field[x + 2, k, half, 40:42, :] = yhi[0, 2 * k:2 * k + 2, lanes]

    def one(k, carry):
        base = 128 - 8 * k
        centre = [field[x + 2, k, half, 8:40, :] for half in range(2)]

        def moved(by):
            rolled = [pltpu.roll(c, by % 128, 1) for c in centre]
            outer = pltpu.roll(side, base + by, 1)
            if by > 0:
                return [
                    jnp.where(lane < by, outer, rolled[0]),
                    jnp.where(lane < by, rolled[0], rolled[1]),
                ]
            return [
                jnp.where(lane >= 128 + by, rolled[1], rolled[0]),
                jnp.where(lane >= 128 + by, outer, rolled[1]),
            ]

        zm1, zm2, zp1, zp2 = moved(1), moved(2), moved(-1), moved(-2)
        for half in range(2):
            u = centre[half]

            def at(dx, dy):
                return field[x + 2 + dx, k, half, 8 + dy:40 + dy, :]

            xp, xm, yp, ym = at(1, 0), at(-1, 0), at(0, 1), at(0, -1)
            zp, zm = zp1[half], zm1[half]
            lap = ((xp + xm) + (yp + ym)) + ((zp + zm) - 6.0 * u)
            flat = (8.0 / 12.0) * (0.2 * (xp - xm) + 0.15 * (yp - ym)) - (1.0 / 12.0) * (
                0.2 * (at(2, 0) - at(-2, 0)) + 0.15 * (at(0, 2) - at(0, -2))
            )
            steep = 8.0 * (zp - zm) - (zp2[half] - zm2[half])
            d = diff[0, :, half * 128:half * 128 + 128]
            new = u + d * lap - (0.3 / 12.0 + (0.02 / 12.0) * u) * steep - flat
            out[k, 0, :, half * 128:half * 128 + 128] = new
        return carry

    lax.fori_loop(0, SNAPS, one, 0)

    xh, xl, yh, yl = [], [], [], []
    for a in range(4):
        for half in range(2):
            high, low = halves(
                field[x + 2, :, half, 8 + 8 * a:16 + 8 * a, :].reshape(128, 128)
            )
            xh.append(high)
            xl.append(low)
            high, low = halves(
                out[:, 0, 8 * a:8 * a + 8, half * 128:half * 128 + 128].reshape(128, 128)
            )
            yh.append(high)
            yl.append(low)
    cat = functools.partial(jnp.concatenate, axis=1)
    total[...] += lax.dot_general(
        jnp.concatenate([cat(yh), cat(yl)], axis=0),
        jnp.concatenate([cat(xh), cat(xl)], axis=0),
        NT, preferred_element_type=F32,
    )

    @pl.when(x == planes - 1)
    def _():
        small = fold(total[...], 2)
        turned = (small[0:16, 0:16] + small[0:16, 16:32]) + (small[16:32, 0:16] + small[16:32, 16:32])
        crossing[...] = pack_square(turned)
        upper, lower_inverse = factor(gram[...])
        norm = jnp.sum(jnp.sum(upper * upper, axis=1, keepdims=True), axis=0, keepdims=True)
        first, second = jacobi_start(upper * lax.rsqrt(norm))

        def turn(step, pair):
            return jacobi_round(*pair)

        first, second = lax.fori_loop(0, SWEEPS * 15, turn, (first, second))
        before[...], after[...], sigmas[...] = spectrum(
            first, second, norm, ncell, upper, lower_inverse
        )


def finish_kernel(sizes, crossing, before, after, reduced, slots, gs, gr):
    enter(sizes)
    turned = unpack_square(sum_over_mesh(sizes, crossing[...], slots, gs, gr))
    inner = lax.dot_general(before[...], turned, NT, precision=HIGH, preferred_element_type=F32)
    reduced[...] = jnp.dot(inner, after[...], precision=HIGH, preferred_element_type=F32)


def shards(sizes, snapshots, diffusivity):
    planes = snapshots.shape[1]
    ncell = float(planes * 32 * 256 * sizes[0] * sizes[1] * sizes[2])
    hbm = pl.BlockSpec(memory_space=pl.ANY)
    vmem = pl.BlockSpec(memory_space=pltpu.VMEM)
    links = sum(count - 1 for count in sizes)
    dma = pltpu.SemaphoreType.DMA
    shape = functools.partial(jax.ShapeDtypeStruct, dtype=F32)
    *halos, gram = pl.pallas_call(
        functools.partial(exchange_kernel, sizes),
        name="exchange",
        out_shape=[
            shape((SNAPS, 2, 32, 256)), shape((SNAPS, 2, 32, 256)),
            shape((planes, 32, 256)), shape((planes, 32, 256)),
            shape((planes, 32, 128)), shape((planes, 32, 128)),
            shape((16, 16)),
        ],
        in_specs=[hbm],
        out_specs=[hbm] * 6 + [vmem],
        scratch_shapes=[
            pltpu.VMEM((planes, SNAPS, 32, 256), F32),
            pltpu.VMEM((planes, 32, 256), F32), pltpu.VMEM((planes, 32, 256), F32),
            pltpu.VMEM((planes, 32, 128), F32), pltpu.VMEM((planes, 32, 128), F32),
            pltpu.VMEM((256, 256), F32), pltpu.VMEM((24, 8, 128), F32),
            dma((planes,)), dma((2,)), dma((2,)), dma((8,)), dma((8,)), dma((8,)), dma((8,)),
            dma((links,)), dma((links,)),
        ],
        compiler_params=pltpu.CompilerParams(
            collective_id=0, has_side_effects=True, vmem_limit_bytes=40 << 20
        ),
    )(snapshots)
    row = lambda *block: pl.BlockSpec((1,) + block, lambda i: (i,) + (0,) * len(block))
    whole = lambda *block: pl.BlockSpec(block, lambda i: (0,) * len(block))
    shifted, crossing, before, after, sigmas = pl.pallas_call(
        functools.partial(shift_kernel, ncell),
        name="shift",
        grid=(planes,),
        out_shape=[
            shape(snapshots.shape), shape((8, 32)), shape((16, 16)), shape((16, 16)), shape((1, 16)),
        ],
        in_specs=[
            hbm, row(32, 256), hbm, hbm, row(32, 256), row(32, 256), row(32, 128), row(32, 128),
            whole(16, 16),
        ],
        out_specs=[
            pl.BlockSpec((SNAPS, 1, 32, 256), lambda i: (0, i, 0, 0)),
            whole(8, 32), whole(16, 16), whole(16, 16), whole(1, 16),
        ],
        scratch_shapes=[
            pltpu.VMEM((planes + 4, SNAPS, 2, 48, 128), F32),
            pltpu.VMEM((256, 256), F32),
            dma((planes + 4, 2)),
        ],
        compiler_params=pltpu.CompilerParams(vmem_limit_bytes=48 << 20),
    )(snapshots, diffusivity, *halos, gram)
    reduced = pl.pallas_call(
        functools.partial(finish_kernel, sizes),
        name="finish",
        out_shape=shape((16, 16)),
        in_specs=[vmem] * 3,
        out_specs=vmem,
        scratch_shapes=[pltpu.VMEM((24, 8, 128), F32), dma((links,)), dma((links,))],
        compiler_params=pltpu.CompilerParams(collective_id=1, has_side_effects=True),
    )(crossing, before, after)
    return (shifted, reduced, sigmas.reshape(16))


def solution(mesh):
    sizes = tuple(mesh.shape[axis] for axis in AXES)
    return jax.shard_map(
        functools.partial(shards, sizes),
        mesh=mesh,
        in_specs=(P(None, "gx", "gy", "gz"), P("gx", "gy", "gz")),
        out_specs=(P(None, "gx", "gy", "gz"), P(), P()),
        check_vma=False,
    )
```

time: 993 us -> 103 us (0.10); the launches traced: 981 us -> 103 us
  local copies, waits for them, and re-layouts: 275 us -> 6.47 us
  waiting for transfers between devices: 213 us -> 0 us
  matrix products: 186 us -> 0 us
  other arithmetic: 139 us -> 0 us
  starting transfers between devices: 99.3 us -> 0 us
  Pallas kernels: 0 us -> 96.1 us
  blocking collectives: 65.1 us -> 0 us
    ppermute x96 -> x0, waiting for transfers between devices: 213 us -> none  [the longest x48 175 us: extended(): lax.ppermute(lax.slice_in_dim(block, block.shape[dim] - width, None, axis...]
    dot_general x638 -> x0, matrix products: 186 us -> none  [the longest x180 30.8 us: turn(): mat = jnp.dot(jnp.dot(rot.T, mat, precision=high), rot, precision=high)]
    gather x271 -> x0, local copies, waits for them, and re-layouts: 174 us -> none  [the longest x90 58.1 us: turn(): aqq = mat[qidx, qidx]]
    ppermute x96 -> x0, starting transfers between devices: 99.3 us -> none  [the longest x48 55.2 us: extended(): lax.ppermute(lax.slice_in_dim(block, block.shape[dim] - width, None, axis...]
    pallas_call x0 -> x3, Pallas kernels: none -> 96.1 us  [the longest x1 52.5 us: shards(): pl.pallas_call(functools.partial(shift_kernel, ncell), name='shift', grid...]
    concatenate x123 -> x0, other arithmetic: 69.5 us -> none  [the longest x90 65.6 us: turn(): app = mat[pidx, pidx]]
    psum x1 -> x0, blocking collectives: 65.1 us -> none  [shards(): gram, cross = lax.psum((gram, cross), ('gx', 'gy', 'gz'))]
    eq x90 -> x0, local copies, waits for them, and re-layouts: 64.9 us -> none  [turn(): onep = jax.nn.one_hot(pidx, count, dtype=jnp.float32)]
  transfers between devices with their start and end apart: 96 -> 0, of which waited for: 84 -> 0; matrix products, arithmetic and copies ran while one was open for 2% -> 0% of each run, Pallas kernels for 0% -> 0%
where the time goes in v1:
time: 103 us
  Pallas kernels  96.1 us (93%)
  local copies, waits for them, and re-layouts  6.47 us (6%)
    pallas_call x1, Pallas kernels, shards(): pl.pallas_call(functools.partial(shift_kernel, ncell), name='shift', grid...  52.5 us
    pallas_call x1, Pallas kernels, shards(): pl.pallas_call(functools.partial(exchange_kernel, sizes), name='exchange'...  29.1 us
    pallas_call x1, Pallas kernels, shards(): pl.pallas_call(functools.partial(finish_kernel, sizes), name='finish', ou...  14.5 us
    unnamed x11, local copies, waits for them, and re-layouts  6.47 us

profile of v1, /device:TPU:0, one launch (start us, length us, event | category | flops | bytes accessed | tf_op | source)
XLA Modules:
  0.0 103.2 jit_solution(15624274182712601817)
XLA Ops:
  0.6 0.0 copy-start
  0.6 3.4 %copy-done = f32[16,16,32,256]{3,2,1,0:T(8,128)S(1)} copy-done((f32[16,16,32,256]{3,2,1,0:T(8,128)S(1)}, f32[16,16,32,256]{3,2,1,0:T(8,128)}, u32[]{:S(2)}) %copy-start) | copy-done | bytes 8388632
  4.0 0.0 copy-start.1
  4.0 29.1 %exchange.1 = (f32[16,2,32,256]{3,2,1,0:T(8,128)S(1)}, f32[16,2,32,256]{3,2,1,0:T(8,128)S(1)}, f32[16,32,256]{2,1,0:T(8,128)S(1)}, f32[16,32,256]{2,1,0:T(8,128)...) custom-call(f32[16,16,32,256]{3,2,1,0:T(8,128)S(1)} %copy-done), custom_call_target="tpu_custom_call" | custom-call | tf_op jit(solution)/shard_map/exchange/pallas_call | solution.py:393
  33.1 0.0 copy-done.1
  33.1 52.5 %shift.1 = (f32[16,16,32,256]{3,2,1,0:T(8,128)}, f32[8,32]{1,0:T(8,128)S(1)}, f32[16,16]{1,0:T(8,128)S(1)}, f32[16,16]{1,0:T(8,128)S(1)}, f32[1,16]{1,0:T(1,128)}) custom-call(f32[16,16,32,256]{3,2,1,0:T(8,128)} %snap.3, f32[16,32,256]{2,1,0:T(8,128)S(1)} %copy-done.1, f32[16,2,32,256]{3,2,1,0:T(8,128)S(1)} %get-tuple-element.15.xlo, ...), custom_call_target="tpu_custom_call" | custom-call | tf_op jit(solution)/shard_map/shift/pallas_call | solution.py:418
  85.6 0.0 copy-start.2
  85.6 0.6 copy-done.2
  86.2 0.0 copy-start.3
  86.2 0.6 copy-done.3
  86.8 0.0 copy-start.4
  86.8 0.6 copy-done.4
  87.4 14.5 %finish.1 = f32[16,16]{1,0:T(8,128)} custom-call(f32[8,32]{1,0:T(8,128)} %copy-done.4, f32[16,16]{1,0:T(8,128)} %copy-done.2, f32[16,16]{1,0:T(8,128)} %copy-done.3), custom_call_target="tpu_custom_call" | custom-call | tf_op jit(solution)/shard_map/finish/pallas_call | solution.py:440
  101.9 1.3 %copy.6 = f32[16,16]{1,0:T(8,128)} copy(f32[16,16]{1,0:T(8,128)} %finish.1) | data formatting | bytes 2048
Async XLA Ops:
  0.6 3.4 %copy-start = (f32[16,16,32,256]{3,2,1,0:T(8,128)S(1)}, f32[16,16,32,256]{3,2,1,0:T(8,128)}, u32[]{:S(2)}) copy-start(f32[16,16,32,256]{3,2,1,0:T(8,128)} %snap.3) | copy-start | bytes 25165828
  4.0 29.1 %copy-start.1 = (f32[16,32,256]{2,1,0:T(8,128)S(1)}, f32[16,32,256]{2,1,0:T(8,128)}, u32[]{:S(2)}) copy-start(f32[16,32,256]{2,1,0:T(8,128)} %diff.1) | copy-start | bytes 1572868
  85.6 0.6 copy-start.2
  86.2 0.6 copy-start.3
  86.8 0.6 copy-start.4

commit v2 on v1

--- a/solution.py
+++ b/solution.py
@@ -242,8 +242,8 @@
 
 def shift_kernel(
     ncell, snap, diff, xlo, xhi, ylo, yhi, zlo, zhi, gram,
-    out, crossing, before, after, sigmas,
-    field, total, sems,
+    out, small, sigmas,
+    field, total, edges, state, factors, sems,
 ):
     x = pl.program_id(0)
     planes = pl.num_programs(0)
@@ -290,52 +290,90 @@
         for half in range(2):
             edge(1, x - (planes - 2), half).wait()
 
-    lane = lax.broadcasted_iota(jnp.int32, (32, 128), 1)
-    group = lane % 8
-    side = jnp.where(group < 4, zhi[0], zlo[0])
+    lane32 = lax.broadcasted_iota(jnp.int32, (32, 128), 1)
+    edges[...] = jnp.where(lane32 % 8 < 4, zhi[0], zlo[0])
     for k in range(SNAPS):
         for half in range(2):
             lanes = pl.ds(half * 128, 128)
             field[x + 2, k, half, 6:8, :] = ylo[0, 2 * k:2 * k + 2, lanes]
             field[x + 2, k, half, 40:42, :] = yhi[0, 2 * k:2 * k + 2, lanes]
 
-    def one(k, carry):
+    lane = lax.broadcasted_iota(jnp.int32, (8, 128), 1)
+
+    def one(k):
         base = 128 - 8 * k
-        centre = [field[x + 2, k, half, 8:40, :] for half in range(2)]
-
-        def moved(by):
-            rolled = [pltpu.roll(c, by % 128, 1) for c in centre]
-            outer = pltpu.roll(side, base + by, 1)
-            if by > 0:
+        for a in range(4):
+            row = 8 + 8 * a
+
+            def at(half, dx=0, dy=0):
+                return field[x + 2 + dx, k, half, row + dy:row + dy + 8, :]
+
+            centre = [at(0), at(1)]
+            side = edges[8 * a:8 * a + 8, :]
+
+            def moved(by):
+                rolled = [pltpu.roll(c, by % 128, 1) for c in centre]
+                outer = pltpu.roll(side, base + by, 1)
+                if by > 0:
+                    return [
+                        jnp.where(lane < by, outer, rolled[0]),
+                        jnp.where(lane < by, rolled[0], rolled[1]),
+                    ]
                 return [
-                    jnp.where(lane < by, outer, rolled[0]),
-                    jnp.where(lane < by, rolled[0], rolled[1]),
+                    jnp.where(lane >= 128 + by, rolled[1], rolled[0]),
+                    jnp.where(lane >= 128 + by, outer, rolled[1]),
                 ]
-            return [
-                jnp.where(lane >= 128 + by, rolled[1], rolled[0]),
-                jnp.where(lane >= 128 + by, outer, rolled[1]),
-            ]
-
-        zm1, zm2, zp1, zp2 = moved(1), moved(2), moved(-1), moved(-2)
-        for half in range(2):
-            u = centre[half]
-
-            def at(dx, dy):
-                return field[x + 2 + dx, k, half, 8 + dy:40 + dy, :]
-
-            xp, xm, yp, ym = at(1, 0), at(-1, 0), at(0, 1), at(0, -1)
-            zp, zm = zp1[half], zm1[half]
-            lap = ((xp + xm) + (yp + ym)) + ((zp + zm) - 6.0 * u)
-            flat = (8.0 / 12.0) * (0.2 * (xp - xm) + 0.15 * (yp - ym)) - (1.0 / 12.0) * (
-                0.2 * (at(2, 0) - at(-2, 0)) + 0.15 * (at(0, 2) - at(0, -2))
-            )
-            steep = 8.0 * (zp - zm) - (zp2[half] - zm2[half])
-            d = diff[0, :, half * 128:half * 128 + 128]
-            new = u + d * lap - (0.3 / 12.0 + (0.02 / 12.0) * u) * steep - flat
-            out[k, 0, :, half * 128:half * 128 + 128] = new
+
+            zp1, zm1, zp2, zm2 = moved(-1), moved(1), moved(-2), moved(2)
+            for half in range(2):
+                u = centre[half]
+                xp, xm, yp, ym = at(half, 1), at(half, -1), at(half, 0, 1), at(half, 0, -1)
+                zp, zm = zp1[half], zm1[half]
+                lap = ((xp + xm) + (yp + ym)) + ((zp + zm) - 6.0 * u)
+                near = (xp - xm) + 0.75 * (yp - ym)
+                far = (at(half, 2) - at(half, -2)) + 0.75 * (at(half, 0, 2) - at(half, 0, -2))
+                steep = 8.0 * (zp - zm) - (zp2[half] - zm2[half])
+                d = diff[0, 8 * a:8 * a + 8, half * 128:half * 128 + 128]
+                new = (u + d * lap) - (0.3 / 12.0 + (0.02 / 12.0) * u) * steep
+                new = new - ((1.6 / 12.0) * near - (0.2 / 12.0) * far)
+                out[k, 0, 8 * a:8 * a + 8, half * 128:half * 128 + 128] = new
+
+    def plain(i, carry):
+        one(2 * i)
+        one(2 * i + 1)
         return carry
 
-    lax.fori_loop(0, SNAPS, one, 0)
+    def turning(i, pair):
+        one(2 * i)
+        one(2 * i + 1)
+        return jacobi_round(*pair)
+
+    @pl.when(x == 0)
+    def _():
+        upper, lower_inverse = factor(gram[...])
+        norm = jnp.sum(jnp.sum(upper * upper, axis=1, keepdims=True), axis=0, keepdims=True)
+        first, second = jacobi_start(upper * lax.rsqrt(norm))
+        state[0:8, 0:32] = first
+        state[8:16, 0:32] = second
+        factors[:, 0:16] = upper
+        factors[:, 16:32] = lower_inverse
+
+    @pl.when(x < planes - 1)
+    def _():
+        first, second = lax.fori_loop(0, 6, turning, (state[0:8, 0:32], state[8:16, 0:32]))
+        state[0:8, 0:32] = first
+        state[8:16, 0:32] = second
+        lax.fori_loop(6, SNAPS // 2, plain, 0)
+
+    @pl.when(x == planes - 1)
+    def _():
+        upper = factors[:, 0:16]
+        lower_inverse = factors[:, 16:32]
+        norm = jnp.sum(jnp.sum(upper * upper, axis=1, keepdims=True), axis=0, keepdims=True)
+        small[0:16, 0:16], small[16:32, 0:16], sigmas[...] = spectrum(
+            state[0:8, 0:32], state[8:16, 0:32], norm, ncell, upper, lower_inverse
+        )
+        lax.fori_loop(0, SNAPS // 2, plain, 0)
 
     xh, xl, yh, yl = [], [], [], []
     for a in range(4):
@@ -359,33 +397,27 @@
 
     @pl.when(x == planes - 1)
     def _():
-        small = fold(total[...], 2)
-        turned = (small[0:16, 0:16] + small[0:16, 16:32]) + (small[16:32, 0:16] + small[16:32, 16:32])
-        crossing[...] = pack_square(turned)
-        upper, lower_inverse = factor(gram[...])
-        norm = jnp.sum(jnp.sum(upper * upper, axis=1, keepdims=True), axis=0, keepdims=True)
-        first, second = jacobi_start(upper * lax.rsqrt(norm))
-
-        def turn(step, pair):
-            return jacobi_round(*pair)
-
-        first, second = lax.fori_loop(0, SWEEPS * 15, turn, (first, second))
-        before[...], after[...], sigmas[...] = spectrum(
-            first, second, norm, ncell, upper, lower_inverse
-        )
-
-
-def finish_kernel(sizes, crossing, before, after, reduced, slots, gs, gr):
+        sums = fold(total[...], 2)
+        turned = (sums[0:16, 0:16] + sums[0:16, 16:32]) + (sums[16:32, 0:16] + sums[16:32, 16:32])
+        small[32:40, 0:32] = pack_square(turned)
+
+
+def finish_kernel(sizes, source, reduced, small, slots, load_sem, gs, gr):
+    load = pltpu.make_async_copy(source, small, load_sem.at[0])
+    load.start()
     enter(sizes)
-    turned = unpack_square(sum_over_mesh(sizes, crossing[...], slots, gs, gr))
-    inner = lax.dot_general(before[...], turned, NT, precision=HIGH, preferred_element_type=F32)
-    reduced[...] = jnp.dot(inner, after[...], precision=HIGH, preferred_element_type=F32)
+    load.wait()
+    turned = unpack_square(sum_over_mesh(sizes, small[32:40, 0:32], slots, gs, gr))
+    inner = lax.dot_general(
+        small[0:16, 0:16], turned, NT, precision=HIGH, preferred_element_type=F32
+    )
+    reduced[...] = jnp.dot(inner, small[16:32, 0:16], precision=HIGH, preferred_element_type=F32)
 
 
 def shards(sizes, snapshots, diffusivity):
     planes = snapshots.shape[1]
     ncell = float(planes * 32 * 256 * sizes[0] * sizes[1] * sizes[2])
-    hbm = pl.BlockSpec(memory_space=pl.ANY)
+    hbm = pl.BlockSpec(memory_space=pltpu.HBM)
     vmem = pl.BlockSpec(memory_space=pltpu.VMEM)
     links = sum(count - 1 for count in sizes)
     dma = pltpu.SemaphoreType.DMA
@@ -410,17 +442,17 @@
             dma((links,)), dma((links,)),
         ],
         compiler_params=pltpu.CompilerParams(
-            collective_id=0, has_side_effects=True, vmem_limit_bytes=40 << 20
+            collective_id=0, has_side_effects=True, vmem_limit_bytes=62 << 20
         ),
     )(snapshots)
     row = lambda *block: pl.BlockSpec((1,) + block, lambda i: (i,) + (0,) * len(block))
     whole = lambda *block: pl.BlockSpec(block, lambda i: (0,) * len(block))
-    shifted, crossing, before, after, sigmas = pl.pallas_call(
+    shifted, small, sigmas = pl.pallas_call(
         functools.partial(shift_kernel, ncell),
         name="shift",
         grid=(planes,),
         out_shape=[
-            shape(snapshots.shape), shape((8, 32)), shape((16, 16)), shape((16, 16)), shape((1, 16)),
+            shape(snapshots.shape), shape((40, 128)), shape((1, 16)),
         ],
         in_specs=[
             hbm, row(32, 256), hbm, hbm, row(32, 256), row(32, 256), row(32, 128), row(32, 128),
@@ -428,24 +460,28 @@
         ],
         out_specs=[
             pl.BlockSpec((SNAPS, 1, 32, 256), lambda i: (0, i, 0, 0)),
-            whole(8, 32), whole(16, 16), whole(16, 16), whole(1, 16),
+            whole(40, 128), whole(1, 16),
         ],
         scratch_shapes=[
             pltpu.VMEM((planes + 4, SNAPS, 2, 48, 128), F32),
-            pltpu.VMEM((256, 256), F32),
+            pltpu.VMEM((256, 256), F32), pltpu.VMEM((32, 128), F32),
+            pltpu.VMEM((16, 128), F32), pltpu.VMEM((16, 128), F32),
             dma((planes + 4, 2)),
         ],
-        compiler_params=pltpu.CompilerParams(vmem_limit_bytes=48 << 20),
+        compiler_params=pltpu.CompilerParams(vmem_limit_bytes=62 << 20),
     )(snapshots, diffusivity, *halos, gram)
     reduced = pl.pallas_call(
         functools.partial(finish_kernel, sizes),
         name="finish",
         out_shape=shape((16, 16)),
-        in_specs=[vmem] * 3,
+        in_specs=[hbm],
         out_specs=vmem,
-        scratch_shapes=[pltpu.VMEM((24, 8, 128), F32), dma((links,)), dma((links,))],
+        scratch_shapes=[
+            pltpu.VMEM((40, 128), F32), pltpu.VMEM((24, 8, 128), F32),
+            dma((1,)), dma((links,)), dma((links,)),
+        ],
         compiler_params=pltpu.CompilerParams(collective_id=1, has_side_effects=True),
-    )(crossing, before, after)
+    )(small)
     return (shifted, reduced, sigmas.reshape(16))
 
 

time: 103 us -> 83.6 us (0.81)
  Pallas kernels: 96.1 us -> 81.5 us
  local copies, waits for them, and re-layouts: 6.47 us -> 1.3 us
    pallas_call x1, Pallas kernels: 52.5 us -> 38.1 us  [shards(): pl.pallas_call(functools.partial(shift_kernel, ncell), name='shift', grid...]
    unnamed x11 -> x1, local copies, waits for them, and re-layouts: 6.47 us -> 1.3 us
where the time goes in v2:
time: 83.6 us; the launch traced here: 83.4 us
  Pallas kernels  81.5 us (97%)
  local copies, waits for them, and re-layouts  1.3 us (2%)
    pallas_call x1, Pallas kernels, shards(): pl.pallas_call(functools.partial(shift_kernel, ncell), name='shift', grid...  38.1 us
    pallas_call x1, Pallas kernels, shards(): pl.pallas_call(functools.partial(exchange_kernel, sizes), name='exchange'...  29.4 us
    pallas_call x1, Pallas kernels, shards(): pl.pallas_call(functools.partial(finish_kernel, sizes), name='finish', ou...  14 us

profile of v2, /device:TPU:0, one launch (start us, length us, event | category | flops | bytes accessed | tf_op | source)
XLA Modules:
  0.0 83.4 jit_solution(15484843142753703023)
XLA Ops:
  0.6 29.4 %exchange.1 = (f32[16,2,32,256]{3,2,1,0:T(8,128)}, f32[16,2,32,256]{3,2,1,0:T(8,128)}, f32[16,32,256]{2,1,0:T(8,128)}, f32[16,32,256]{2,1,0:T(8,128)}, f32[16,32...) custom-call(f32[16,16,32,256]{3,2,1,0:T(8,128)} %snap.3), custom_call_target="tpu_custom_call" | custom-call | tf_op jit(solution)/shard_map/exchange/pallas_call | solution.py:425
  30.1 38.1 %shift.1 = (f32[16,16,32,256]{3,2,1,0:T(8,128)}, f32[40,128]{1,0:T(8,128)}, f32[1,16]{1,0:T(1,128)}) custom-call(f32[16,16,32,256]{3,2,1,0:T(8,128)} %snap.3, f32[16,32,256]{2,1,0:T(8,128)} %diff.1, f32[16,2,32,256]{3,2,1,0:T(8,128)} %get-tuple-element.13.xlo, f32[16,2,32,256]{3,2,1,0:T(8,128)} %get-tuple-element.14.xhi, ...), custom_call_target="tpu_custom_call" | custom-call | tf_op jit(solution)/shard_map/shift/pallas_call | solution.py:450
  68.1 14.0 %finish.1 = f32[16,16]{1,0:T(8,128)} custom-call(f32[40,128]{1,0:T(8,128)} %get-tuple-element.21.source), custom_call_target="tpu_custom_call" | custom-call | tf_op jit(solution)/shard_map/finish/pallas_call | solution.py:473
  82.1 1.3 %copy.6 = f32[16,16]{1,0:T(8,128)} copy(f32[16,16]{1,0:T(8,128)} %finish.1) | data formatting | bytes 2048

commit v3 on v0

v3 whole, which is shorter than its diff:
```python
import functools

import jax
import jax.numpy as jnp
import numpy as np
from jax import lax
from jax.experimental import pallas as pl
from jax.experimental.pallas import tpu as pltpu
from jax.sharding import PartitionSpec as P

SNAPS = 16
RANK = 12
SWEEPS = 6
HIGH = lax.Precision.HIGHEST
F32 = jnp.float32
BF16 = jnp.bfloat16
MESH = pl.DeviceIdType.MESH
AXES = ("gx", "gy", "gz")


def peers(sizes):
    found = []
    for axis, count in zip(AXES, sizes):
        for step in range(1, count):
            found.append((axis, lax.rem(lax.axis_index(axis) + step, count)))
    return found


def pack_square(square):
    return jnp.concatenate([square[0:8], square[8:16]], axis=1)


def unpack_square(packed):
    return jnp.concatenate([packed[:, 0:16], packed[:, 16:32]], axis=0)


def stage_copies(sizes, place, slots, send_sems, recv_sems):
    axis, count = AXES[place], sizes[place]
    me = lax.axis_index(axis)
    at = sum(size - 1 for size in sizes[:place])
    return [
        pltpu.make_async_remote_copy(
            src_ref=slots.at[8 * place + me],
            dst_ref=slots.at[8 * place + me],
            send_sem=send_sems.at[at + step - 1],
            recv_sem=recv_sems.at[at + step - 1],
            device_id={axis: lax.rem(me + step, count)},
            device_id_type=MESH,
        )
        for step in range(1, count)
    ]


def stage_start(sizes, place, value, slots, send_sems, recv_sems):
    slots[8 * place + lax.axis_index(AXES[place]), :, 0:32] = value
    for copy in stage_copies(sizes, place, slots, send_sems, recv_sems):
        copy.start()


def stage_finish(sizes, place, slots, send_sems, recv_sems):
    for copy in stage_copies(sizes, place, slots, send_sems, recv_sems):
        copy.wait()
    value = slots[8 * place, :, 0:32]
    for slot in range(1, sizes[place]):
        value = value + slots[8 * place + slot, :, 0:32]
    return value


def halves(block):
    high = block.astype(BF16)
    return high, (block - high.astype(F32)).astype(BF16)


def fold(total, groups):
    sub = lax.broadcasted_iota(jnp.int32, (8, 256), 0)
    lane = lax.broadcasted_iota(jnp.int32, (8, 256), 1)
    same = (sub == lane % 8).astype(F32)
    rows = jnp.sum(total.reshape(groups * 16, 8, 256) * same[None], axis=1)
    pick = (
        lax.broadcasted_iota(jnp.int32, (256, 32), 0) // 8
        == lax.broadcasted_iota(jnp.int32, (256, 32), 1)
    ).astype(F32)
    return jnp.dot(rows, pick, precision=HIGH, preferred_element_type=F32)


NT = (((1,), (1,)), ((), ()))
TN = (((0,), (0,)), ((), ()))


def factor(gram):
    row = lax.broadcasted_iota(jnp.int32, (16, 32), 0)
    col = lax.broadcasted_iota(jnp.int32, (16, 32), 1)
    mat = jnp.concatenate([gram, (row == col).astype(F32)[:, 0:16]], axis=1)
    for j in range(16):
        scale = lax.rsqrt(mat[j:j + 1, j:j + 1])
        top = mat[j:j + 1, :] * scale
        side = jnp.where(row[:, 0:1] > j, mat[:, j:j + 1] * scale, 0.0)
        mat = jnp.where(row == j, top, mat - side * top)
    upper = jnp.where(col[:, 0:16] >= row[:, 0:16], mat[:, 0:16], 0.0)
    return upper, mat[:, 16:32]


def jacobi_round(first, second):
    lane = lax.broadcasted_iota(jnp.int32, (8, 32), 1)
    sub = lax.broadcasted_iota(jnp.int32, (8, 32), 0)
    inside = lane < 16
    masked_first = jnp.where(inside, first, 0.0)
    masked_second = jnp.where(inside, second, 0.0)
    app = jnp.sum(masked_first * first, axis=1, keepdims=True)
    aqq = jnp.sum(masked_second * second, axis=1, keepdims=True)
    apq = jnp.sum(masked_first * second, axis=1, keepdims=True)
    tau = aqq - app
    square = tau * tau + 4.0 * apq * apq
    live = square > 0
    inverse = lax.rsqrt(jnp.where(live, square, 1.0))
    cos2 = 0.5 + 0.5 * jnp.abs(tau) * inverse
    root = lax.rsqrt(cos2)
    cosine = jnp.where(live, cos2 * root, 1.0)
    signed = jnp.where(tau >= 0, apq, -apq)
    sine = jnp.where(live, signed * inverse * root, 0.0)
    new_first = cosine * first - sine * second
    new_second = sine * first + cosine * second
    down = pltpu.roll(new_first, 1, 0)
    up = pltpu.roll(new_second, 7, 0)
    entering = pltpu.roll(new_second, 1, 0)
    top = jnp.where(sub == 0, new_first, jnp.where(sub == 1, entering, down))
    bottom = jnp.where(sub == 7, new_first, up)
    return top, bottom


def jacobi_start(upper):
    eye = (
        lax.broadcasted_iota(jnp.int32, (16, 16), 0) == lax.broadcasted_iota(jnp.int32, (16, 16), 1)
    ).astype(F32)
    both = jnp.concatenate([upper, eye], axis=1)
    return both[0:8], jnp.concatenate([both[i:i + 1] for i in range(15, 7, -1)], axis=0)


def spectrum(first, second, norm, ncell, upper, lower_inverse):
    both = jnp.concatenate([first, second], axis=0)
    scaled = both[:, 0:16]
    vecs = both[:, 16:32]
    lam = jnp.sum(scaled * scaled, axis=1, keepdims=True)
    row = lax.broadcasted_iota(jnp.int32, (16, 16), 0)
    col = lax.broadcasted_iota(jnp.int32, (16, 16), 1)
    along = jnp.sum(jnp.where(row == col, lam, 0.0), axis=0, keepdims=True)
    above = (along > lam).astype(F32)
    ties = ((along == lam) & (col < row)).astype(F32)
    greater = jnp.sum(above, axis=1, keepdims=True)
    keep = (greater < RANK - 0.5).astype(F32)
    place = greater + jnp.sum(ties, axis=1, keepdims=True)
    sigma = jnp.sqrt(lam * (norm / ncell))
    sigmas = jnp.sum(jnp.where(place == col.astype(F32), sigma, 0.0), axis=0, keepdims=True)
    proj = lax.dot_general(vecs * keep, vecs, TN, precision=HIGH, preferred_element_type=F32)
    weights = keep / (lam * norm)
    inverse = lax.dot_general(vecs * weights, vecs, TN, precision=HIGH, preferred_element_type=F32)
    before = jnp.dot(proj, lower_inverse, precision=HIGH, preferred_element_type=F32)
    after = lax.dot_general(upper, inverse, TN, precision=HIGH, preferred_element_type=F32)
    return before, after, sigmas


def slope_weights():
    base = np.zeros((260, 512), np.float32)
    for z in range(256):
        for step, lap, slope in ((-2, 0, 1), (-1, 1, -8), (0, -6, 0), (1, 1, 8), (2, 0, -1)):
            base[z + step + 2, z] += lap
            base[z + step + 2, 256 + z] += slope
    edge = base[[258, 259, 0, 1]]
    group = np.concatenate([edge, edge])
    return np.concatenate([base[2:258], base[2:258]] + [group] * 16)


JACOBI_AT = 8


def step_kernel(
    sizes, ncell, snap, diff, slope, out, reduced, sigmas,
    field, split, zbuf, weights, yplo, yphi, zplo, zphi, ylo, yhi, zlo, zhi, dbuf, obuf,
    gtotal, ctotal, state, factors, gslots, cslots,
    load_sem, aux_sem, out_sem, xs, xr, ys, yr, zs, zr, gs, gr, cs, cr,
):
    planes = dbuf.shape[0]
    parts = 4
    each = planes // parts

    def load(x, half):
        lanes = pl.ds(half * 128, 128)
        return pltpu.make_async_copy(
            snap.at[:, x, :, lanes], field.at[x + 2, :, half, pl.ds(8, 32)], load_sem.at[x, half]
        )

    for x in range(planes):
        for half in range(2):
            load(x, half).start()
    slope_copy = pltpu.make_async_copy(slope, weights, aux_sem.at[0])
    diff_copy = pltpu.make_async_copy(diff, dbuf, aux_sem.at[1])
    slope_copy.start()
    diff_copy.start()

    barrier = pltpu.get_barrier_semaphore()
    known = peers(sizes)
    for axis, target in known:
        pl.semaphore_signal(barrier, inc=1, device_id={axis: target}, device_id_type=MESH)
    near = {}
    for axis, count in zip(AXES, sizes):
        me = lax.axis_index(axis)
        near[axis] = (lax.rem(me + count - 1, count), lax.rem(me + 1, count))

    def remote(src, dst, send, recv, axis, side):
        return pltpu.make_async_remote_copy(
            src_ref=src, dst_ref=dst, send_sem=send, recv_sem=recv,
            device_id={axis: near[axis][side]}, device_id_type=MESH,
        )

    def x_copies():
        found = []
        for side in range(2):
            for p in range(2):
                for half in range(2):
                    source = p if side == 0 else planes - 2 + p
                    slot = planes + 2 + p if side == 0 else p
                    at = 4 * side + 2 * p + half
                    found.append(remote(
                        snap.at[:, source, :, pl.ds(half * 128, 128)],
                        field.at[slot, :, half, pl.ds(8, 32)],
                        xs.at[at], xr.at[at], "gx", side,
                    ))
        return found

    def yz_copies(part):
        span = pl.ds(part * each, each)
        a, b = 2 * part, 2 * part + 1
        return [
            remote(yplo.at[span], yhi.at[span], ys.at[a], yr.at[a], "gy", 0),
            remote(yphi.at[span], ylo.at[span], ys.at[b], yr.at[b], "gy", 1),
            remote(zplo.at[span], zhi.at[span], zs.at[a], zr.at[a], "gz", 0),
            remote(zphi.at[span], zlo.at[span], zs.at[b], zr.at[b], "gz", 1),
        ]

    lane = lax.broadcasted_iota(jnp.int32, (32, 128), 1)

    def pack(x, carry):
        for half in range(2):
            load(x, half).wait()
        left = jnp.zeros((32, 128), F32)
        right = jnp.zeros((32, 128), F32)
        for k in range(SNAPS):
            for half in range(2):
                lanes = pl.ds(half * 128, 128)
                yplo[x, 2 * k:2 * k + 2, lanes] = field[x + 2, k, half, 8:10, :]
                yphi[x, 2 * k:2 * k + 2, lanes] = field[x + 2, k, half, 38:40, :]
            head = field[x + 2, k, 0, 8:40, :]
            tail = pltpu.roll(field[x + 2, k, 1, 8:40, :], (8 * k + 4) % 128, 1)
            if k:
                head = pltpu.roll(head, 8 * k, 1)
            left = jnp.where((lane >= 8 * k) & (lane < 8 * k + 2), head, left)
            right = jnp.where((lane >= 8 * k + 2) & (lane < 8 * k + 4), tail, right)
        zplo[x] = left
        zphi[x] = right
        return carry

    def inner(x, carry):
        for a in range(4):
            for half in range(2):
                high, low = halves(
                    field[x + 2, :, half, 8 + 8 * a:16 + 8 * a, :].reshape(128, 128)
                )
                split[x, a, 0:128, half * 128:half * 128 + 128] = high
                split[x, a, 128:256, half * 128:half * 128 + 128] = low
        both = jnp.concatenate([split[x, a] for a in range(4)], axis=1)
        gtotal[...] += lax.dot_general(both, both, NT, preferred_element_type=F32)
        return carry

    gtotal[...] = jnp.zeros_like(gtotal)
    ctotal[...] = jnp.zeros_like(ctotal)
    for part in range(parts):
        lax.fori_loop(part * each, (part + 1) * each, pack, 0)
        if part == 0:
            pl.semaphore_wait(barrier, len(known))
            for copy in x_copies():
                copy.start()
        for copy in yz_copies(part):
            copy.start()
    lax.fori_loop(0, planes, inner, 0)
    sums = fold(gtotal[...], 2)
    mine = (sums[0:16, 0:16] + sums[16:32, 16:32]) + (sums[0:16, 16:32] + sums[16:32, 0:16])
    gram_args = (gslots, gs, gr)
    cross_args = (cslots, cs, cr)
    stage_start(sizes, 0, pack_square(mine), *gram_args)
    slope_copy.wait()
    diff_copy.wait()

    def write(x, slot):
        return pltpu.make_async_copy(obuf.at[slot], out.at[:, x], out_sem.at[slot])

    group = lax.broadcasted_iota(jnp.int32, (SNAPS, 8, 128), 0)
    own = lax.broadcasted_iota(jnp.int32, (SNAPS, 8, 128), 2) // 8 == group

    def rotate(rounds):
        first, second = lax.fori_loop(
            0, rounds, lambda i, pair: jacobi_round(*pair), (state[0:8, 0:32], state[8:16, 0:32])
        )
        state[0:8, 0:32] = first
        state[8:16, 0:32] = second

    def plane(i, carry):
        x = lax.rem(i + 2, planes)
        slot = lax.rem(i, 2)

        @pl.when(i == 0)
        def _():
            for copy in yz_copies(0):
                copy.wait()

        for part in range(1, parts):
            @pl.when(i == part * each - 2)
            def _(part=part):
                for copy in yz_copies(part):
                    copy.wait()

        @pl.when(i == planes - 4)
        def _():
            for copy in x_copies():
                copy.wait()

        @pl.when(i == JACOBI_AT - 6)
        def _():
            stage_start(sizes, 1, stage_finish(sizes, 0, *gram_args), *gram_args)

        @pl.when(i == JACOBI_AT - 3)
        def _():
            stage_start(sizes, 2, stage_finish(sizes, 1, *gram_args), *gram_args)

        @pl.when(i == JACOBI_AT)
        def _():
            upper, lower_inverse = factor(unpack_square(stage_finish(sizes, 2, *gram_args)))
            norm = jnp.sum(jnp.sum(upper * upper, axis=1, keepdims=True), axis=0, keepdims=True)
            first, second = jacobi_start(upper * lax.rsqrt(norm))
            state[0:8, 0:32] = first
            state[8:16, 0:32] = second
            factors[:, 0:16] = upper
            factors[:, 16:32] = lower_inverse

        @pl.when(i >= 2)
        def _():
            write(lax.rem(x + planes - 2, planes), slot).wait()

        outer = jnp.where(lane % 8 < 2, zhi[x], zlo[x])
        top = outer.astype(BF16).astype(F32)
        outer = jnp.where(lane % 8 < 4, top, pltpu.roll(outer - top, 4, 1))
        rows = []
        for a in range(4):
            edge = jnp.where(own, outer[8 * a:8 * a + 8, :][None], 0.0)
            rows.append(jnp.concatenate(
                [split[x, a, 0:128], split[x, a, 128:256], edge.reshape(128, 128).astype(BF16)],
                axis=1,
            ))
        zbuf[...] = jnp.dot(
            jnp.concatenate(rows, axis=0), weights[...], preferred_element_type=F32
        )
        for k in range(SNAPS):
            for half in range(2):
                lanes = pl.ds(half * 128, 128)
                field[x + 2, k, half, 6:8, :] = ylo[x, 2 * k:2 * k + 2, lanes]
                field[x + 2, k, half, 40:42, :] = yhi[x, 2 * k:2 * k + 2, lanes]

        def one(k):
            for a in range(4):
                row = 8 + 8 * a
                at_z = pl.ds(pl.multiple_of(128 * a + 8 * k, 8), 8)
                for half in range(2):
                    def at(dx, dy):
                        return field[x + 2 + dx, k, half, row + dy:row + dy + 8, :]

                    lanes = pl.ds(half * 128, 128)
                    u = at(0, 0)
                    xp, xm, yp, ym = at(1, 0), at(-1, 0), at(0, 1), at(0, -1)
                    lap = ((xp + xm) + (yp + ym)) + zbuf[at_z, lanes]
                    close = (xp - xm) + 0.75 * (yp - ym)
                    far = (at(2, 0) - at(-2, 0)) + 0.75 * (at(0, 2) - at(0, -2))
                    steep = zbuf[at_z, pl.ds(256 + half * 128, 128)]
                    new = (u + dbuf[x, 8 * a:8 * a + 8, lanes] * lap) - (
                        0.3 / 12.0 + (0.02 / 12.0) * u
                    ) * steep
                    new = new - ((1.6 / 12.0) * close - (0.2 / 12.0) * far)
                    obuf[slot, k, 8 * a:8 * a + 8, lanes] = new

        def plain(j, carry):
            one(2 * j)
            one(2 * j + 1)
            return carry

        def turning(j, pair):
            one(2 * j)
            one(2 * j + 1)
            return jacobi_round(*pair)

        @pl.when(i < JACOBI_AT)
        def _():
            lax.fori_loop(0, SNAPS // 2, plain, 0)

        @pl.when(i >= JACOBI_AT)
        def _():
            first, second = lax.fori_loop(
                0, SNAPS // 2, turning, (state[0:8, 0:32], state[8:16, 0:32])
            )
            state[0:8, 0:32] = first
            state[8:16, 0:32] = second

        write(x, slot).start()
        yh, yl = [], []
        for a in range(4):
            high, low = halves(obuf[slot, :, 8 * a:8 * a + 8, :].reshape(128, 256))
            yh.append(high)
            yl.append(low)
        cat = functools.partial(jnp.concatenate, axis=1)
        ctotal[...] += lax.dot_general(
            jnp.concatenate([cat(yh), cat(yl)], axis=0),
            cat([split[x, a] for a in range(4)]),
            NT, preferred_element_type=F32,
        )
        return carry

    lax.fori_loop(0, planes, plane, 0)
    left_over = SWEEPS * 15 - (planes - JACOBI_AT) * (SNAPS // 2)
    sums = fold(ctotal[...], 2)
    turned = (sums[0:16, 0:16] + sums[0:16, 16:32]) + (sums[16:32, 0:16] + sums[16:32, 16:32])
    stage_start(sizes, 0, pack_square(turned), *cross_args)
    rotate(left_over // 2)
    stage_start(sizes, 1, stage_finish(sizes, 0, *cross_args), *cross_args)
    rotate(left_over - left_over // 2)
    stage_start(sizes, 2, stage_finish(sizes, 1, *cross_args), *cross_args)
    upper = factors[:, 0:16]
    norm = jnp.sum(jnp.sum(upper * upper, axis=1, keepdims=True), axis=0, keepdims=True)
    before, after, sigmas[...] = spectrum(
        state[0:8, 0:32], state[8:16, 0:32], norm, ncell, upper, factors[:, 16:32]
    )
    for slot in range(2):
        write(slot, slot).wait()
    turned = unpack_square(stage_finish(sizes, 2, *cross_args))
    middle = lax.dot_general(before, turned, NT, precision=HIGH, preferred_element_type=F32)
    reduced[...] = jnp.dot(middle, after, precision=HIGH, preferred_element_type=F32)


def shards(sizes, snapshots, diffusivity):
    planes = snapshots.shape[1]
    ncell = float(planes * 32 * 256 * sizes[0] * sizes[1] * sizes[2])
    hbm = pl.BlockSpec(memory_space=pltpu.HBM)
    vmem = pl.BlockSpec(memory_space=pltpu.VMEM)
    links = sum(count - 1 for count in sizes)
    dma = pltpu.SemaphoreType.DMA
    shape = functools.partial(jax.ShapeDtypeStruct, dtype=F32)
    rows = [pltpu.VMEM((planes, 32, width), F32) for width in (256, 256, 128, 128)]
    shifted, reduced, sigmas = pl.pallas_call(
        functools.partial(step_kernel, sizes, ncell),
        name="step",
        out_shape=[shape(snapshots.shape), shape((16, 16)), shape((1, 16))],
        in_specs=[hbm] * 3,
        out_specs=[hbm, vmem, vmem],
        scratch_shapes=[
            pltpu.VMEM((planes + 4, SNAPS, 2, 48, 128), F32),
            pltpu.VMEM((planes, 4, 256, 256), BF16),
            pltpu.VMEM((512, 512), F32),
            pltpu.VMEM((640, 512), BF16),
            *rows,
            *rows,
            pltpu.VMEM((planes, 32, 256), F32),
            pltpu.VMEM((2, SNAPS, 32, 256), F32),
            pltpu.VMEM((256, 256), F32), pltpu.VMEM((256, 256), F32),
            pltpu.VMEM((16, 128), F32), pltpu.VMEM((16, 128), F32),
            pltpu.VMEM((24, 8, 128), F32), pltpu.VMEM((24, 8, 128), F32),
            dma((planes, 2)), dma((2,)), dma((2,)),
            *[dma((8,))] * 6,
            *[dma((links,))] * 4,
        ],
        compiler_params=pltpu.CompilerParams(
            collective_id=0, has_side_effects=True, vmem_limit_bytes=62 << 20
        ),
    )(snapshots, diffusivity, jnp.asarray(slope_weights(), BF16))
    return (shifted, reduced, sigmas.reshape(16))


def solution(mesh):
    sizes = tuple(mesh.shape[axis] for axis in AXES)
    return jax.shard_map(
        functools.partial(shards, sizes),
        mesh=mesh,
        in_specs=(P(None, "gx", "gy", "gz"), P("gx", "gy", "gz")),
        out_specs=(P(None, "gx", "gy", "gz"), P(), P()),
        check_vma=False,
    )
```

time: 993 us -> 73.3 us (0.07); the launches traced: 981 us -> 73.2 us
  local copies, waits for them, and re-layouts: 275 us -> 9.56 us
  waiting for transfers between devices: 213 us -> 0 us
  matrix products: 186 us -> 0 us
  other arithmetic: 139 us -> 0 us
  starting transfers between devices: 99.3 us -> 0 us
  blocking collectives: 65.1 us -> 0 us
  Pallas kernels: 0 us -> 63 us
    ppermute x96 -> x0, waiting for transfers between devices: 213 us -> none  [the longest x48 175 us: extended(): lax.ppermute(lax.slice_in_dim(block, block.shape[dim] - width, None, axis...]
    dot_general x638 -> x0, matrix products: 186 us -> none  [the longest x180 30.8 us: turn(): mat = jnp.dot(jnp.dot(rot.T, mat, precision=high), rot, precision=high)]
    gather x271 -> x0, local copies, waits for them, and re-layouts: 174 us -> none  [the longest x90 58.1 us: turn(): aqq = mat[qidx, qidx]]
    ppermute x96 -> x0, starting transfers between devices: 99.3 us -> none  [the longest x48 55.2 us: extended(): lax.ppermute(lax.slice_in_dim(block, block.shape[dim] - width, None, axis...]
    concatenate x123 -> x0, other arithmetic: 69.5 us -> none  [the longest x90 65.6 us: turn(): app = mat[pidx, pidx]]
    psum x1 -> x0, blocking collectives: 65.1 us -> none  [shards(): gram, cross = lax.psum((gram, cross), ('gx', 'gy', 'gz'))]
    eq x90 -> x0, local copies, waits for them, and re-layouts: 64.9 us -> none  [turn(): onep = jax.nn.one_hot(pidx, count, dtype=jnp.float32)]
    pallas_call x0 -> x1, Pallas kernels: none -> 63 us  [shards(): pl.pallas_call(functools.partial(step_kernel, sizes, ncell), name='step',...]
  transfers between devices with their start and end apart: 96 -> 0, of which waited for: 84 -> 0; matrix products, arithmetic and copies ran while one was open for 2% -> 0% of each run, Pallas kernels for 0% -> 0%
where the time goes in v3:
time: 73.3 us; the launch traced here: 73.2 us
  Pallas kernels  63 us (86%)
  local copies, waits for them, and re-layouts  9.56 us (13%)
    pallas_call x1, Pallas kernels, shards(): pl.pallas_call(functools.partial(step_kernel, sizes, ncell), name='step',...  63 us
    unnamed x7, local copies, waits for them, and re-layouts  9.56 us

profile of v3, /device:TPU:0, one launch (start us, length us, event | category | flops | bytes accessed | tf_op | source)
XLA Modules:
  0.0 73.2 jit_solution(1282011194023121786)
XLA Ops:
  0.6 63.0 %step.1 = (f32[16,16,32,256]{3,2,1,0:T(8,128)}, f32[16,16]{1,0:T(8,128)}, f32[1,16]{1,0:T(1,128)}) custom-call(f32[16,16,32,256]{3,2,1,0:T(8,128)} %snap.1, f32[16,32,256]{2,1,0:T(8,128)} %diff.1, bf16[640,512]{1,0:T(8,128)(2,1)} %constant.2.clone.slope), custom_call_target="tpu_custom_call" | custom-call | tf_op jit(solution)/shard_map/step/pallas_call | solution.py:454
  63.6 0.0 copy-start
  63.6 0.0 copy-start.1
  63.6 8.4 %copy.9 = f32[16,16,32,256]{3,2,1,0:T(8,128)} copy(f32[16,16,32,256]{3,2,1,0:T(8,128)} %get-tuple-element.12) | data formatting | bytes 16777216
  72.1 0.0 copy-done
  72.1 0.6 copy.10
  72.7 0.0 copy-done.1
  72.7 0.5 copy.11
Async XLA Ops:
  63.6 8.5 %copy-start = (f32[16,16]{1,0:T(8,128)S(1)}, f32[16,16]{1,0:T(8,128)}, u32[]{:S(2)}) copy-start(f32[16,16]{1,0:T(8,128)} %get-tuple-element.13) | copy-start | bytes 3076
  63.6 9.1 %copy-start.1 = (f32[1,16]{1,0:T(1,128)S(1)}, f32[1,16]{1,0:T(1,128)}, u32[]{:S(2)}) copy-start(f32[1,16]{1,0:T(1,128)} %get-tuple-element.8) | copy-start | bytes 196

commit v4 on v3

--- a/solution.py
+++ b/solution.py
@@ -160,22 +160,22 @@
 
 
 def slope_weights():
-    base = np.zeros((260, 512), np.float32)
-    for z in range(256):
+    base = np.zeros((132, 256), np.float32)
+    for z in range(128):
         for step, lap, slope in ((-2, 0, 1), (-1, 1, -8), (0, -6, 0), (1, 1, 8), (2, 0, -1)):
             base[z + step + 2, z] += lap
-            base[z + step + 2, 256 + z] += slope
-    edge = base[[258, 259, 0, 1]]
-    group = np.concatenate([edge, edge])
-    return np.concatenate([base[2:258], base[2:258]] + [group] * 16)
+            base[z + step + 2, 128 + z] += slope
+    edge = base[[0, 1, 130, 131]]
+    places = (np.arange(128) + 2) % 4
+    return np.concatenate([base[2:130], base[2:130], edge[places]])
 
 
 JACOBI_AT = 8
 
 
 def step_kernel(
-    sizes, ncell, snap, diff, slope, out, reduced, sigmas,
-    field, split, zbuf, weights, yplo, yphi, zplo, zphi, ylo, yhi, zlo, zhi, dbuf, obuf,
+    sizes, ncell, snap, diff, slope, out, small,
+    field, split, zbuf, ybuf, weights, yplo, yphi, zplo, zphi, ylo, yhi, zlo, zhi, mid, dbuf, obuf,
     gtotal, ctotal, state, factors, gslots, cslots,
     load_sem, aux_sem, out_sem, xs, xr, ys, yr, zs, zr, gs, gr, cs, cr,
 ):
@@ -244,6 +244,7 @@
             load(x, half).wait()
         left = jnp.zeros((32, 128), F32)
         right = jnp.zeros((32, 128), F32)
+        centre = jnp.zeros((32, 128), F32)
         for k in range(SNAPS):
             for half in range(2):
                 lanes = pl.ds(half * 128, 128)
@@ -255,11 +256,12 @@
                 head = pltpu.roll(head, 8 * k, 1)
             left = jnp.where((lane >= 8 * k) & (lane < 8 * k + 2), head, left)
             right = jnp.where((lane >= 8 * k + 2) & (lane < 8 * k + 4), tail, right)
+            centre = jnp.where((lane >= 8 * k + 4) & (lane < 8 * k + 6), tail, centre)
+            low = (8 * k - 2) % 128
+            centre = jnp.where((lane >= low) & (lane < low + 2), head, centre)
         zplo[x] = left
         zphi[x] = right
-        return carry
-
-    def inner(x, carry):
+        mid[x] = centre
         for a in range(4):
             for half in range(2):
                 high, low = halves(
@@ -273,6 +275,7 @@
 
     gtotal[...] = jnp.zeros_like(gtotal)
     ctotal[...] = jnp.zeros_like(ctotal)
+    ybuf[...] = jnp.zeros_like(ybuf)
     for part in range(parts):
         lax.fori_loop(part * each, (part + 1) * each, pack, 0)
         if part == 0:
@@ -281,7 +284,6 @@
                 copy.start()
         for copy in yz_copies(part):
             copy.start()
-    lax.fori_loop(0, planes, inner, 0)
     sums = fold(gtotal[...], 2)
     mine = (sums[0:16, 0:16] + sums[16:32, 16:32]) + (sums[0:16, 16:32] + sums[16:32, 0:16])
     gram_args = (gslots, gs, gr)
@@ -294,7 +296,7 @@
         return pltpu.make_async_copy(obuf.at[slot], out.at[:, x], out_sem.at[slot])
 
     group = lax.broadcasted_iota(jnp.int32, (SNAPS, 8, 128), 0)
-    own = lax.broadcasted_iota(jnp.int32, (SNAPS, 8, 128), 2) // 8 == group
+    own = (lax.broadcasted_iota(jnp.int32, (SNAPS, 8, 128), 2) + 2) % 128 // 8 == group
 
     def rotate(rounds):
         first, second = lax.fori_loop(
@@ -302,6 +304,13 @@
         )
         state[0:8, 0:32] = first
         state[8:16, 0:32] = second
+
+    def cross(x):
+        cat = functools.partial(jnp.concatenate, axis=1)
+        ctotal[...] += lax.dot_general(
+            cat([ybuf[a] for a in range(4)]), cat([split[x, a] for a in range(4)]),
+            NT, preferred_element_type=F32,
+        )
 
     def plane(i, carry):
         x = lax.rem(i + 2, planes)
@@ -345,16 +354,28 @@
         def _():
             write(lax.rem(x + planes - 2, planes), slot).wait()
 
-        outer = jnp.where(lane % 8 < 2, zhi[x], zlo[x])
+        cross(lax.rem(i + 1, planes))
+        place = lane % 8
+        outer = jnp.where(place < 2, zhi[x], jnp.where(place < 4, zlo[x], mid[x]))
         top = outer.astype(BF16).astype(F32)
-        outer = jnp.where(lane % 8 < 4, top, pltpu.roll(outer - top, 4, 1))
+        rest = outer - top
+        inside = (place >= 2) & (place < 6)
+        outer = [
+            jnp.where(inside, top, pltpu.roll(rest, 124, 1)),
+            jnp.where(inside, pltpu.roll(rest, 4, 1), top),
+        ]
         rows = []
-        for a in range(4):
-            edge = jnp.where(own, outer[8 * a:8 * a + 8, :][None], 0.0)
-            rows.append(jnp.concatenate(
-                [split[x, a, 0:128], split[x, a, 128:256], edge.reshape(128, 128).astype(BF16)],
-                axis=1,
-            ))
+        for half in range(2):
+            lanes = pl.ds(half * 128, 128)
+            for a in range(4):
+                edge = jnp.where(own, outer[half][8 * a:8 * a + 8, :][None], 0.0)
+                rows.append(jnp.concatenate(
+                    [
+                        split[x, a, 0:128, lanes], split[x, a, 128:256, lanes],
+                        edge.reshape(128, 128).astype(BF16),
+                    ],
+                    axis=1,
+                ))
         zbuf[...] = jnp.dot(
             jnp.concatenate(rows, axis=0), weights[...], preferred_element_type=F32
         )
@@ -364,35 +385,43 @@
                 field[x + 2, k, half, 6:8, :] = ylo[x, 2 * k:2 * k + 2, lanes]
                 field[x + 2, k, half, 40:42, :] = yhi[x, 2 * k:2 * k + 2, lanes]
 
-        def one(k):
+        def one(k, a, half):
+            row = 8 + 8 * a
+            at_z = pl.ds(pl.multiple_of(512 * half + 128 * a + 8 * k, 8), 8)
+
+            def at(dx, dy):
+                return field[x + 2 + dx, k, half, row + dy:row + dy + 8, :]
+
+            lanes = pl.ds(half * 128, 128)
+            u = at(0, 0)
+            xp, xm, yp, ym = at(1, 0), at(-1, 0), at(0, 1), at(0, -1)
+            lap = ((xp + xm) + (yp + ym)) + zbuf[at_z, 0:128]
+            close = (xp - xm) + 0.75 * (yp - ym)
+            far = (at(2, 0) - at(-2, 0)) + 0.75 * (at(0, 2) - at(0, -2))
+            new = (u + dbuf[x, 8 * a:8 * a + 8, lanes] * lap) - (
+                0.3 / 12.0 + (0.02 / 12.0) * u
+            ) * zbuf[at_z, 128:256]
+            new = new - ((1.6 / 12.0) * close - (0.2 / 12.0) * far)
+            obuf[slot, k, 8 * a:8 * a + 8, lanes] = new
+            return new
+
+        def fields(j):
+            k = 2 * j
             for a in range(4):
-                row = 8 + 8 * a
-                at_z = pl.ds(pl.multiple_of(128 * a + 8 * k, 8), 8)
                 for half in range(2):
-                    def at(dx, dy):
-                        return field[x + 2 + dx, k, half, row + dy:row + dy + 8, :]
-
                     lanes = pl.ds(half * 128, 128)
-                    u = at(0, 0)
-                    xp, xm, yp, ym = at(1, 0), at(-1, 0), at(0, 1), at(0, -1)
-                    lap = ((xp + xm) + (yp + ym)) + zbuf[at_z, lanes]
-                    close = (xp - xm) + 0.75 * (yp - ym)
-                    far = (at(2, 0) - at(-2, 0)) + 0.75 * (at(0, 2) - at(0, -2))
-                    steep = zbuf[at_z, pl.ds(256 + half * 128, 128)]
-                    new = (u + dbuf[x, 8 * a:8 * a + 8, lanes] * lap) - (
-                        0.3 / 12.0 + (0.02 / 12.0) * u
-                    ) * steep
-                    new = new - ((1.6 / 12.0) * close - (0.2 / 12.0) * far)
-                    obuf[slot, k, 8 * a:8 * a + 8, lanes] = new
+                    high, low = halves(
+                        jnp.concatenate([one(k, a, half), one(k + 1, a, half)], axis=0)
+                    )
+                    ybuf[a, pl.ds(pl.multiple_of(8 * k, 16), 16), lanes] = high
+                    ybuf[a, pl.ds(pl.multiple_of(128 + 8 * k, 16), 16), lanes] = low
 
         def plain(j, carry):
-            one(2 * j)
-            one(2 * j + 1)
+            fields(j)
             return carry
 
         def turning(j, pair):
-            one(2 * j)
-            one(2 * j + 1)
+            fields(j)
             return jacobi_round(*pair)
 
         @pl.when(i < JACOBI_AT)
@@ -408,20 +437,10 @@
             state[8:16, 0:32] = second
 
         write(x, slot).start()
-        yh, yl = [], []
-        for a in range(4):
-            high, low = halves(obuf[slot, :, 8 * a:8 * a + 8, :].reshape(128, 256))
-            yh.append(high)
-            yl.append(low)
-        cat = functools.partial(jnp.concatenate, axis=1)
-        ctotal[...] += lax.dot_general(
-            jnp.concatenate([cat(yh), cat(yl)], axis=0),
-            cat([split[x, a] for a in range(4)]),
-            NT, preferred_element_type=F32,
-        )
         return carry
 
     lax.fori_loop(0, planes, plane, 0)
+    cross(1)
     left_over = SWEEPS * 15 - (planes - JACOBI_AT) * (SNAPS // 2)
     sums = fold(ctotal[...], 2)
     turned = (sums[0:16, 0:16] + sums[0:16, 16:32]) + (sums[16:32, 0:16] + sums[16:32, 16:32])
@@ -432,14 +451,26 @@
     stage_start(sizes, 2, stage_finish(sizes, 1, *cross_args), *cross_args)
     upper = factors[:, 0:16]
     norm = jnp.sum(jnp.sum(upper * upper, axis=1, keepdims=True), axis=0, keepdims=True)
-    before, after, sigmas[...] = spectrum(
+    before, after, small[16:17, 0:16] = spectrum(
         state[0:8, 0:32], state[8:16, 0:32], norm, ncell, upper, factors[:, 16:32]
     )
     for slot in range(2):
         write(slot, slot).wait()
     turned = unpack_square(stage_finish(sizes, 2, *cross_args))
     middle = lax.dot_general(before, turned, NT, precision=HIGH, preferred_element_type=F32)
-    reduced[...] = jnp.dot(middle, after, precision=HIGH, preferred_element_type=F32)
+    small[0:16, 0:16] = jnp.dot(middle, after, precision=HIGH, preferred_element_type=F32)
+
+
+def emit_kernel(held, small, out, reduced, sigmas, sem):
+    copies = [
+        pltpu.make_async_copy(held.at[k], out.at[k], sem.at[k]) for k in range(SNAPS)
+    ]
+    for copy in copies:
+        copy.start()
+    reduced[...] = small[0:16, 0:16]
+    sigmas[...] = small[16:17, 0:16]
+    for copy in copies:
+        copy.wait()
 
 
 def shards(sizes, snapshots, diffusivity):
@@ -451,19 +482,21 @@
     dma = pltpu.SemaphoreType.DMA
     shape = functools.partial(jax.ShapeDtypeStruct, dtype=F32)
     rows = [pltpu.VMEM((planes, 32, width), F32) for width in (256, 256, 128, 128)]
-    shifted, reduced, sigmas = pl.pallas_call(
+    held, small = pl.pallas_call(
         functools.partial(step_kernel, sizes, ncell),
         name="step",
-        out_shape=[shape(snapshots.shape), shape((16, 16)), shape((1, 16))],
+        out_shape=[shape(snapshots.shape), shape((24, 128))],
         in_specs=[hbm] * 3,
-        out_specs=[hbm, vmem, vmem],
+        out_specs=[pl.BlockSpec(memory_space=pl.ANY), vmem],
         scratch_shapes=[
             pltpu.VMEM((planes + 4, SNAPS, 2, 48, 128), F32),
             pltpu.VMEM((planes, 4, 256, 256), BF16),
-            pltpu.VMEM((512, 512), F32),
-            pltpu.VMEM((640, 512), BF16),
+            pltpu.VMEM((1024, 256), F32),
+            pltpu.VMEM((4, 256, 256), BF16),
+            pltpu.VMEM((384, 256), BF16),
             *rows,
             *rows,
+            pltpu.VMEM((planes, 32, 128), F32),
             pltpu.VMEM((planes, 32, 256), F32),
             pltpu.VMEM((2, SNAPS, 32, 256), F32),
             pltpu.VMEM((256, 256), F32), pltpu.VMEM((256, 256), F32),
@@ -474,9 +507,22 @@
             *[dma((links,))] * 4,
         ],
         compiler_params=pltpu.CompilerParams(
-            collective_id=0, has_side_effects=True, vmem_limit_bytes=62 << 20
+            collective_id=0, has_side_effects=True, vmem_limit_bytes=42 << 20
         ),
-    )(snapshots, diffusivity, jnp.asarray(slope_weights(), BF16))
+    )(
+        snapshots,
+        pltpu.with_memory_space_constraint(diffusivity, pltpu.HBM),
+        pltpu.with_memory_space_constraint(jnp.asarray(slope_weights(), BF16), pltpu.HBM),
+    )
+    shifted, reduced, sigmas = pl.pallas_call(
+        emit_kernel,
+        name="emit",
+        out_shape=[shape(snapshots.shape), shape((16, 16)), shape((1, 16))],
+        in_specs=[pl.BlockSpec(memory_space=pl.ANY), vmem],
+        out_specs=[hbm, vmem, vmem],
+        scratch_shapes=[dma((SNAPS,))],
+        compiler_params=pltpu.CompilerParams(vmem_limit_bytes=4 << 20),
+    )(held, small)
     return (shifted, reduced, sigmas.reshape(16))
 
 

time: 73.3 us -> 61.4 us (0.84)
  local copies, waits for them, and re-layouts: 9.56 us -> 0 us
  Pallas kernels: 63 us -> 60.6 us
    unnamed x7 -> x0, local copies, waits for them, and re-layouts: 9.56 us -> none
    pallas_call x1, Pallas kernels: 63 us -> 56.6 us  [shards(): pl.pallas_call(functools.partial(step_kernel, sizes, ncell), name='step',...]
    pallas_call x0 -> x1, Pallas kernels: none -> 4.02 us  [shards(): pl.pallas_call(emit_kernel, name='emit', out_shape=[shape(snapshots.shape...]
where the time goes in v4:
time: 61.4 us; the launch traced here: 61.3 us
  Pallas kernels  60.6 us (99%)
  between operations  0.64 us (1%)
    pallas_call x1, Pallas kernels, shards(): pl.pallas_call(functools.partial(step_kernel, sizes, ncell), name='step',...  56.6 us
    pallas_call x1, Pallas kernels, shards(): pl.pallas_call(emit_kernel, name='emit', out_shape=[shape(snapshots.shape...  4.02 us

profile of v4, /device:TPU:0, one launch (start us, length us, event | category | flops | bytes accessed | tf_op | source)
XLA Modules:
  0.0 61.3 jit_solution(530319841795733069)
XLA Ops:
  0.6 56.6 %step.1 = (f32[16,16,32,256]{3,2,1,0:T(8,128)S(1)}, f32[24,128]{1,0:T(8,128)S(1)}) custom-call(f32[16,16,32,256]{3,2,1,0:T(8,128)} %snap.1, f32[16,32,256]{2,1,0:T(8,128)} %diff.1, bf16[384,256]{1,0:T(8,128)(2,1)} %constant.2.clone.slope), custom_call_target="tpu_custom_call" | custom-call | tf_op jit(solution)/shard_map/step/pallas_call | solution.py:485
  57.3 4.0 %emit.1 = (f32[16,16,32,256]{3,2,1,0:T(8,128)}, f32[16,16]{1,0:T(8,128)}, f32[1,16]{1,0:T(1,128)}) custom-call(f32[16,16,32,256]{3,2,1,0:T(8,128)S(1)} %get-tuple-element.8.held, f32[24,128]{1,0:T(8,128)S(1)} %get-tuple-element.9.small), custom_call_target="tpu_custom_call" | custom-call | tf_op jit(solution)/shard_map/emit/pallas_call | solution.py:517

commit v5 on v4

--- a/solution.py
+++ b/solution.py
@@ -170,7 +170,7 @@
     return np.concatenate([base[2:130], base[2:130], edge[places]])
 
 
-JACOBI_AT = 8
+JACOBI_AT = 11
 
 
 def step_kernel(

time: 61.4 us -> 56.8 us (0.925)
  Pallas kernels: 60.6 us -> 56 us
    pallas_call x1, Pallas kernels: 56.6 us -> 52 us  [shards(): pl.pallas_call(functools.partial(step_kernel, sizes, ncell), name='step',...]
where the time goes in v5:
time: 56.8 us; the launch traced here: 56.7 us
  Pallas kernels  56 us (99%)
  between operations  0.64 us (1%)
    pallas_call x1, Pallas kernels, shards(): pl.pallas_call(functools.partial(step_kernel, sizes, ncell), name='step',...  52 us
    pallas_call x1, Pallas kernels, shards(): pl.pallas_call(emit_kernel, name='emit', out_shape=[shape(snapshots.shape...  4.02 us

profile of v5, /device:TPU:0, one launch (start us, length us, event | category | flops | bytes accessed | tf_op | source)
XLA Modules:
  0.0 56.7 jit_solution(6747263142743036633)
XLA Ops:
  0.6 52.0 %step.1 = (f32[16,16,32,256]{3,2,1,0:T(8,128)S(1)}, f32[24,128]{1,0:T(8,128)S(1)}) custom-call(f32[16,16,32,256]{3,2,1,0:T(8,128)} %snap.1, f32[16,32,256]{2,1,0:T(8,128)} %diff.1, bf16[384,256]{1,0:T(8,128)(2,1)} %constant.2.clone.slope), custom_call_target="tpu_custom_call" | custom-call | tf_op jit(solution)/shard_map/step/pallas_call | solution.py:485
  52.6 4.0 %emit.1 = (f32[16,16,32,256]{3,2,1,0:T(8,128)}, f32[16,16]{1,0:T(8,128)}, f32[1,16]{1,0:T(1,128)}) custom-call(f32[16,16,32,256]{3,2,1,0:T(8,128)S(1)} %get-tuple-element.8.held, f32[24,128]{1,0:T(8,128)S(1)} %get-tuple-element.9.small), custom_call_target="tpu_custom_call" | custom-call | tf_op jit(solution)/shard_map/emit/pallas_call | solution.py:517

commit v6 on v5

--- a/solution.py
+++ b/solution.py
@@ -170,7 +170,7 @@
     return np.concatenate([base[2:130], base[2:130], edge[places]])
 
 
-JACOBI_AT = 11
+JACOBI_AT = 13
 
 
 def step_kernel(
@@ -332,11 +332,11 @@
             for copy in x_copies():
                 copy.wait()
 
-        @pl.when(i == JACOBI_AT - 6)
+        @pl.when(i == JACOBI_AT - 5)
         def _():
             stage_start(sizes, 1, stage_finish(sizes, 0, *gram_args), *gram_args)
 
-        @pl.when(i == JACOBI_AT - 3)
+        @pl.when(i == JACOBI_AT - 2)
         def _():
             stage_start(sizes, 2, stage_finish(sizes, 1, *gram_args), *gram_args)
 
@@ -445,10 +445,12 @@
     sums = fold(ctotal[...], 2)
     turned = (sums[0:16, 0:16] + sums[0:16, 16:32]) + (sums[16:32, 0:16] + sums[16:32, 16:32])
     stage_start(sizes, 0, pack_square(turned), *cross_args)
-    rotate(left_over // 2)
+    early, middle = left_over * 4 // 9, left_over // 3
+    rotate(early)
     stage_start(sizes, 1, stage_finish(sizes, 0, *cross_args), *cross_args)
-    rotate(left_over - left_over // 2)
+    rotate(middle)
     stage_start(sizes, 2, stage_finish(sizes, 1, *cross_args), *cross_args)
+    rotate(left_over - early - middle)
     upper = factors[:, 0:16]
     norm = jnp.sum(jnp.sum(upper * upper, axis=1, keepdims=True), axis=0, keepdims=True)
     before, after, small[16:17, 0:16] = spectrum(

time: 56.8 us -> 54.1 us (0.952)
  Pallas kernels: 56 us -> 53.3 us
    pallas_call x1, Pallas kernels: 52 us -> 49.3 us  [shards(): pl.pallas_call(functools.partial(step_kernel, sizes, ncell), name='step',...]
where the time goes in v6:
time: 54.1 us; the launch traced here: 54 us
  Pallas kernels  53.3 us (99%)
  between operations  0.64 us (1%)
    pallas_call x1, Pallas kernels, shards(): pl.pallas_call(functools.partial(step_kernel, sizes, ncell), name='step',...  49.3 us
    pallas_call x1, Pallas kernels, shards(): pl.pallas_call(emit_kernel, name='emit', out_shape=[shape(snapshots.shape...  4.02 us

profile of v6, /device:TPU:0, one launch (start us, length us, event | category | flops | bytes accessed | tf_op | source)
XLA Modules:
  0.0 54.0 jit_solution(2700103023731250501)
XLA Ops:
  0.6 49.3 %step.1 = (f32[16,16,32,256]{3,2,1,0:T(8,128)S(1)}, f32[24,128]{1,0:T(8,128)S(1)}) custom-call(f32[16,16,32,256]{3,2,1,0:T(8,128)} %snap.1, f32[16,32,256]{2,1,0:T(8,128)} %diff.1, bf16[384,256]{1,0:T(8,128)(2,1)} %constant.2.clone.slope), custom_call_target="tpu_custom_call" | custom-call | tf_op jit(solution)/shard_map/step/pallas_call | solution.py:487
  49.9 4.0 %emit.1 = (f32[16,16,32,256]{3,2,1,0:T(8,128)}, f32[16,16]{1,0:T(8,128)}, f32[1,16]{1,0:T(1,128)}) custom-call(f32[16,16,32,256]{3,2,1,0:T(8,128)S(1)} %get-tuple-element.8.held, f32[24,128]{1,0:T(8,128)S(1)} %get-tuple-element.9.small), custom_call_target="tpu_custom_call" | custom-call | tf_op jit(solution)/shard_map/emit/pallas_call | solution.py:519

commit v7 on v6

--- a/solution.py
+++ b/solution.py
@@ -417,7 +417,8 @@
                     ybuf[a, pl.ds(pl.multiple_of(128 + 8 * k, 16), 16), lanes] = low
 
         def plain(j, carry):
-            fields(j)
+            fields(2 * j)
+            fields(2 * j + 1)
             return carry
 
         def turning(j, pair):
@@ -426,7 +427,7 @@
 
         @pl.when(i < JACOBI_AT)
         def _():
-            lax.fori_loop(0, SNAPS // 2, plain, 0)
+            lax.fori_loop(0, SNAPS // 4, plain, 0)
 
         @pl.when(i >= JACOBI_AT)
         def _():

time: 54.1 us -> 53.9 us (level)
  no operation moved by 1% of the time
where the time goes in v7:
time: 53.9 us; the launch traced here: 53.8 us
  Pallas kernels  53.2 us (99%)
  between operations  0.64 us (1%)
    pallas_call x1, Pallas kernels, shards(): pl.pallas_call(functools.partial(step_kernel, sizes, ncell), name='step',...  49.2 us
    pallas_call x1, Pallas kernels, shards(): pl.pallas_call(emit_kernel, name='emit', out_shape=[shape(snapshots.shape...  4.02 us

profile of v7, /device:TPU:0, one launch (start us, length us, event | category | flops | bytes accessed | tf_op | source)
XLA Modules:
  0.0 53.8 jit_solution(7772712624682145972)
XLA Ops:
  0.6 49.2 %step.1 = (f32[16,16,32,256]{3,2,1,0:T(8,128)S(1)}, f32[24,128]{1,0:T(8,128)S(1)}) custom-call(f32[16,16,32,256]{3,2,1,0:T(8,128)} %snap.1, f32[16,32,256]{2,1,0:T(8,128)} %diff.1, bf16[384,256]{1,0:T(8,128)(2,1)} %constant.2.clone.slope), custom_call_target="tpu_custom_call" | custom-call | tf_op jit(solution)/shard_map/step/pallas_call | solution.py:488
  49.8 4.0 %emit.1 = (f32[16,16,32,256]{3,2,1,0:T(8,128)}, f32[16,16]{1,0:T(8,128)}, f32[1,16]{1,0:T(1,128)}) custom-call(f32[16,16,32,256]{3,2,1,0:T(8,128)S(1)} %get-tuple-element.8.held, f32[24,128]{1,0:T(8,128)S(1)} %get-tuple-element.9.small), custom_call_target="tpu_custom_call" | custom-call | tf_op jit(solution)/shard_map/emit/pallas_call | solution.py:520
